TPU v7x, 32 devices: a whole 2x2x4 slice. The times are simulated.
32 devices in a mesh: rep: 4 (over y, x), exp: 8 (over z, core).
Axes of the slice: x: 2, y: 2, z: 4, core: 2. Of those that a mesh axis runs over, the one named last changes fastest.
Arguments:
- tokens: bfloat16 [4096, 1024], P(('rep', 'exp')), may hold values from -6 to 6
- gain: float32 [1024], replicated, may hold values from 0.1 to 1.9
- expert_ids: int32 [4096, 2], P(('rep', 'exp')), may hold values from 0 to 7, all different within a row
- gates: float32 [4096, 2], P(('rep', 'exp')), may hold values from 0.1 to 0.9
- w_in: bfloat16 [8, 1024, 4096], P('exp', None, 'rep'), may hold values from -0.1875 to 0.1875
- w_out: bfloat16 [8, 4096, 1024], P('exp', 'rep'), may hold values from -0.09375 to 0.09375
- cotangent: bfloat16 [4096, 1024], P(('rep', 'exp')), may hold values from -6 to 6
Outputs:
- mixed: bfloat16 [4096, 1024], P(('rep', 'exp'))
- grad_tokens: bfloat16 [4096, 1024], P(('rep', 'exp'))
- grad_in: bfloat16 [8, 1024, 4096], P('exp', None, 'rep')
- grad_out: bfloat16 [8, 4096, 1024], P('exp', 'rep')
Inputs may be any that keep to these rules, and one draw needn't show every extreme that they name: `expert_ids`: each token names two different experts, and every expert is named by some token.
All inputs are finite; a program needn't handle non-finite values.
Results may differ from a plain program's by a relative error of at most 0.007.
Values may be sent and summed in bfloat16 or wider, within the bound.
No kernel may reach another device: no remote copies, remote signals or barrier semaphores. Data moves between devices by JAX's collectives and lax.ppermute only.
A program may use at most 64 MiB of HBM per device.

v0:
```python
import functools

import jax
import jax.numpy as jnp
from jax import lax
from jax.experimental import pallas as pl
from jax.experimental.pallas import tpu as pltpu
from jax.sharding import PartitionSpec as P


epsilon = 1e-05
ROOT_2_PI = 0.7978845608028654
CUBIC = 0.044715
BF16, F32 = jnp.bfloat16, jnp.float32
GATHER = (2, 2, 2, 2)
SCATTER = (2, 2, 2, 2)


def normalize(entries, gain):
    center = entries - jnp.mean(entries, axis=-1, keepdims=True)
    spread = jnp.mean(center * center, axis=-1, keepdims=True)
    return center * lax.rsqrt(spread + epsilon) * gain


def activate(entries):
    return jax.nn.gelu(entries, approximate=True)


def slot_table(expert_ids, experts, capacity):
    flattened = expert_ids.reshape(-1)
    labels = jnp.arange(experts, dtype=jnp.int32)
    onehot = (flattened[:, None] == labels[None, :]).astype(jnp.int32)
    before = jnp.cumsum(onehot, axis=0) - onehot
    ranking = jnp.sum(before * onehot, axis=1)
    target = jnp.where(ranking < capacity, flattened * capacity + ranking, -1)
    places = jnp.arange(experts * capacity, dtype=jnp.int32)
    return (target[None, :] == places[:, None]).astype(BF16)


def place_rows(select, paired, experts, capacity):
    packed = jnp.dot(select, paired, preferred_element_type=F32).astype(BF16)
    return packed.reshape(experts, capacity, paired.shape[1])


def take_rows(select, landed):
    flattened = landed.reshape(-1, landed.shape[-1])
    return jnp.einsum("sp,sd->pd", select, flattened, preferred_element_type=F32)


def arrive(sent):
    landed = lax.all_to_all(sent, "exp", split_axis=0, concat_axis=0, tiled=True)
    return lax.all_gather(landed.reshape(-1, landed.shape[-1]), "rep", axis=0, tiled=True)


def depart(partial_value, experts, capacity):
    summed = lax.psum_scatter(partial_value.astype(BF16), "rep", scatter_dimension=0, tiled=True)
    return lax.all_to_all(
        summed.reshape(experts, capacity, summed.shape[-1]),
        "exp",
        split_axis=0,
        concat_axis=0,
        tiled=True,
    )


def local_general(tokens, gain, expert_ids, gates, w_in, w_out, cotangent):
    experts = lax.axis_size("exp")
    tok_count, features = tokens.shape
    capacity = max(2, 2 * tok_count // experts)
    values = tokens.astype(F32)
    normed, norm_back = jax.vjp(lambda entries: normalize(entries, gain), values)
    normed = normed.astype(BF16)
    select = slot_table(expert_ids, experts, capacity)
    x_sent = place_rows(select, jnp.repeat(normed, 2, axis=0), experts, capacity)
    scaled = (cotangent.astype(F32)[:, None, :] * gates[:, :, None]).astype(BF16)
    d_sent = place_rows(select, scaled.reshape(2 * tok_count, features), experts, capacity)
    w_first, w_second = w_in[0], w_out[0]
    in_rows = arrive(x_sent)
    preact = jnp.dot(in_rows, w_first, preferred_element_type=F32)
    activated, act_back = jax.vjp(activate, preact)
    hidden = activated.astype(BF16)
    y_back = depart(jnp.dot(hidden, w_second, preferred_element_type=F32), experts, capacity)
    grad_rows = arrive(d_sent)
    d_hidden = jnp.einsum("rd,fd->rf", grad_rows, w_second, preferred_element_type=F32)
    d_pre = act_back(d_hidden)[0].astype(BF16)
    grad_second = jnp.einsum("rf,rd->fd", hidden, grad_rows, preferred_element_type=F32)
    grad_first = jnp.einsum("rd,rf->df", in_rows, d_pre, preferred_element_type=F32)
    d_back = depart(
        jnp.einsum("rf,df->rd", d_pre, w_first, preferred_element_type=F32), experts, capacity
    )
    returned = take_rows(select, y_back).reshape(tok_count, 2, features)
    mixed = (values + jnp.sum(gates[:, :, None] * returned, axis=1)).astype(BF16)
    d_normed = jnp.sum(take_rows(select, d_back).reshape(tok_count, 2, features), axis=1)
    grad_tokens = (cotangent.astype(F32) + norm_back(d_normed)[0]).astype(BF16)
    return (mixed, grad_tokens, grad_first.astype(BF16)[None], grad_second.astype(BF16)[None])


def dot_nn(a, b):
    return jnp.dot(a, b, preferred_element_type=F32)


def dot_nt(a, b):
    return lax.dot_general(a, b, (((1,), (1,)), ((), ())), preferred_element_type=F32)


def dot_tn(a, b):
    return lax.dot_general(a, b, (((0,), (0,)), ((), ())), preferred_element_type=F32)


def slots_of(ids, me, experts, capacity):
    count = ids[0].shape[0]
    chips = experts // 2
    lanes = lax.broadcasted_iota(jnp.int32, (count, 128), 1)
    hit = [(i == lanes).astype(F32) for i in ids]
    row = lax.broadcasted_iota(jnp.int32, (count, count), 0)
    col = lax.broadcasted_iota(jnp.int32, (count, count), 1)
    before = dot_nn((col < row).astype(BF16), (hit[0] + hit[1]).astype(BF16))
    slots = []
    for k in range(2):
        rank = jnp.sum(before * hit[k], axis=1, keepdims=True).astype(jnp.int32)
        label = ids[k] ^ me
        block = (label & 1) * chips + (label >> 1)
        slots.append(jnp.where(rank < capacity, block * capacity + rank, -1))
    return slots


def row_stats(values):
    center = values - jnp.mean(values, axis=-1, keepdims=True)
    spread = jnp.mean(center * center, axis=-1, keepdims=True)
    return center, lax.rsqrt(spread + epsilon)


def column(row):
    size = row.shape[1]
    here = lax.broadcasted_iota(jnp.int32, (size, size), 0) == lax.broadcasted_iota(jnp.int32, (size, size), 1)
    return jnp.sum(jnp.where(here, row, 0.0), axis=1, keepdims=True)


def send_kernel(experts, capacity, me_ref, *refs):
    sources, (keep_ref, swap_ref, slot_ref, gate_ref) = refs[:5], refs[5:9]
    landing, sems = refs[9:14], refs[14]
    copies = [pltpu.make_async_copy(a, b, sems.at[i]) for i, (a, b) in enumerate(zip(sources, landing))]
    for c in copies:
        c.start()
    id_rows, gate_rows, tok_ref, gain_ref, cot_ref = landing
    count, features = tok_ref.shape
    half = experts // 2 * capacity
    copies[0].wait()
    ids = [column(id_rows[k : k + 1, :].astype(F32)).astype(jnp.int32) for k in range(2)]
    slots = slots_of(ids, me_ref[0], experts, capacity)
    lane = lax.broadcasted_iota(jnp.int32, (count, 2 * half), 1)
    picks = [(slots[k] == lane).astype(F32) for k in range(2)]
    second = lax.broadcasted_iota(jnp.int32, (count, 2), 1) == 1
    slot_ref[...] = jnp.where(second, slots[1], slots[0])
    copies[1].wait()
    gates = [column(gate_rows[k : k + 1, :]) for k in range(2)]
    gate_ref[...] = jnp.where(second, gates[1], gates[0])
    copies[2].wait()
    copies[3].wait()
    center, scale = row_stats(tok_ref[...].astype(F32))
    normed = (center * scale * gain_ref[...]).astype(BF16)
    copies[4].wait()
    cot = cot_ref[...].astype(F32)
    scaled = jnp.concatenate([(cot * g).astype(BF16) for g in gates], axis=0)
    pick_x = (picks[0] + picks[1]).astype(BF16)
    pick_d = jnp.concatenate([p.astype(BF16) for p in picks], axis=0)
    for part, out in ((1, swap_ref), (0, keep_ref)):
        at = slice(part * half, (part + 1) * half)
        out[:, :features] = dot_tn(pick_x[:, at], normed).astype(BF16)
        out[:, features:] = dot_tn(pick_d[:, at], scaled).astype(BF16)


def expert_kernel(pieces, form, *refs):
    parts, (w1_ref, w2_ref), outs = refs[:pieces], refs[pieces : pieces + 2], refs[pieces + 2 : -2]
    hid_ref, pre_ref = refs[-2:]
    count, width = parts[0].shape
    features = width // 2
    hidden_units = w1_ref.shape[1]
    tile = min(256, hidden_units)
    x_rows = jnp.concatenate([p[:, :features] for p in parts], axis=0)
    d_rows = jnp.concatenate([p[:, features:] for p in parts], axis=0)
    for j in range(0, hidden_units, tile):
        at = slice(j, j + tile)
        v = dot_nn(x_rows, w1_ref[:, at])
        dh = dot_nt(d_rows, w2_ref[at, :])
        v2 = v * v
        t = jnp.tanh(v * (ROOT_2_PI + (ROOT_2_PI * CUBIC) * v2))
        hid_ref[:, at] = (0.5 * v * (1.0 + t)).astype(BF16)
        slope = 0.5 * (1.0 + t) + 0.5 * v * (1.0 - t * t) * (ROOT_2_PI + (3.0 * ROOT_2_PI * CUBIC) * v2)
        pre_ref[:, at] = (dh * slope).astype(BF16)
    hid, pre = hid_ref[...], pre_ref[...]
    half = count // 2
    if form == 2:
        moves = (
            (0, 0, count, 0, 0),
            (1, 0, half, 1, 0),
            (3, 0, half, 1, half),
            (2, half, count, 2, 0),
            (3, half, count, 2, half),
            (2, 0, half, 3, 0),
            (1, half, count, 4, 0),
        )
    else:
        near, then = (2, 1) if form == 0 else (1, 2)
        moves = ((0, 0, count, 0, 0), (near, 0, count, 1, 0), (3, 0, count, 1, count), (then, 0, count, 2, 0))
    for j in range(0, features, tile):
        y = dot_nn(hid, w2_ref[:, j : j + tile]).astype(BF16)
        dx = dot_nt(pre, w1_ref[j : j + tile, :]).astype(BF16)
        for rep, low, high, out, to in moves:
            rows, there = slice(rep * count + low, rep * count + high), slice(to, to + high - low)
            outs[out][there, j : j + tile] = y[rows]
            outs[out][there, features + j : features + j + tile] = dx[rows]


def grad_kernel(pieces, chips, first, *refs):
    rows, tall, out_ref = refs[:pieces], refs[pieces : pieces + chips], refs[pieces + chips]
    step = pl.program_id(0)
    tile = out_ref.shape[0]
    features = rows[0].shape[1] // 2
    at = pl.ds(pl.multiple_of(step * tile, tile), tile)
    if first:
        left = jnp.concatenate([r[:, at] for r in rows], axis=0)
        right = jnp.concatenate([r[...] for r in tall], axis=0)
    else:
        left = jnp.concatenate([r[:, at] for r in tall], axis=0)
        right = jnp.concatenate([r[:, features:] for r in rows], axis=0)
    out_ref[...] = dot_tn(left, right).astype(BF16)


def last_kernel(capacity, slot_ref, tok_ref, gain_ref, gate_ref, cot_ref, *refs):
    pieces, other_ref, mixed_ref, grad_ref = refs[:-3], refs[-3], refs[-2], refs[-1]
    count, features = tok_ref.shape
    own = jnp.concatenate([p[:capacity] for p in pieces], axis=0)
    returned = jnp.concatenate([own, other_ref[...]], axis=0)
    lane = lax.broadcasted_iota(jnp.int32, (count, returned.shape[0]), 1)
    picks = [(slot_ref[:, k : k + 1] == lane).astype(F32) for k in range(2)]
    values = tok_ref[...].astype(F32)
    total = None
    for k in range(2):
        term = gate_ref[:, k : k + 1] * dot_nn(picks[k].astype(BF16), returned[:, :features])
        total = term if total is None else total + term
    mixed_ref[...] = (values + total).astype(BF16)
    d_normed = dot_nn((picks[0] + picks[1]).astype(BF16), returned[:, features:])
    center, scale = row_stats(values)
    down = d_normed * gain_ref[...]
    along = jnp.sum(down * center, axis=-1, keepdims=True) * (1.0 / features)
    d_center = down * scale - center * (scale * scale * scale * along)
    d_values = d_center - jnp.mean(d_center, axis=-1, keepdims=True)
    grad_ref[...] = (cot_ref[...].astype(F32) + d_values).astype(BF16)


def vmem(array):
    return pltpu.with_memory_space_constraint(array, pltpu.VMEM)


def call(kernel, outs, args, limit=24, **kwargs):
    spec = pl.BlockSpec(memory_space=pltpu.VMEM)
    return pl.pallas_call(
        kernel,
        out_shape=tuple(pltpu.VMEM(s, d) for s, d in outs),
        in_specs=[spec] * len(args),
        out_specs=tuple(spec for _ in outs),
        compiler_params=pltpu.CompilerParams(vmem_limit_bytes=limit << 20),
        **kwargs,
    )(*[vmem(a) for a in args])


def flip(array, axis_name, mask):
    size = lax.axis_size(axis_name)
    return lax.ppermute(array, axis_name, [(i, i ^ mask) for i in range(size)])


def f32(array):
    return array.astype(F32)


def local(tokens, gain, expert_ids, gates, w_in, w_out, cotangent):
    return local_inner(tokens, gain, expert_ids, gates, w_in, w_out, cotangent)


def local_inner(tokens, gain, expert_ids, gates, w_in, w_out, cotangent):
    experts = lax.axis_size("exp")
    chips = experts // 2
    tok_count, features = tokens.shape
    capacity = max(2, 2 * tok_count // experts)
    me = lax.axis_index("exp").astype(jnp.int32).reshape(1)
    gain_row = gain.reshape(1, features)
    wide = 2 * features
    half = chips * capacity
    count = 2 * capacity
    spec = pl.BlockSpec(memory_space=pltpu.VMEM)
    there = [pltpu.with_memory_space_constraint(a, pltpu.HBM) for a in (expert_ids.T, gates.T, tokens, gain_row, cotangent)]
    keep, swap, slots, gate_columns = pl.pallas_call(
        functools.partial(send_kernel, experts, capacity),
        out_shape=(
            pltpu.VMEM((half, wide), BF16),
            pltpu.VMEM((half, wide), BF16),
            pltpu.VMEM((tok_count, 2), jnp.int32),
            pltpu.VMEM((tok_count, 2), F32),
        ),
        in_specs=[pl.BlockSpec(memory_space=pltpu.SMEM)] + [pl.BlockSpec(memory_space=pltpu.HBM)] * 5,
        out_specs=(spec,) * 4,
        scratch_shapes=[pltpu.VMEM(a.shape, a.dtype) for a in there] + [pltpu.SemaphoreType.DMA((5,))],
        compiler_params=pltpu.CompilerParams(vmem_limit_bytes=16 << 20),
        name="send",
    )(me, *there)
    swapped = flip(swap, "exp", 1)
    w_first, w_second = w_in[0], w_out[0]
    units = w_first.shape[1]
    landed = {}
    for k in range(chips):
        at = slice(k * capacity, (k + 1) * capacity)
        own = jnp.concatenate([keep[at], swapped[at]], axis=0)
        landed[k] = flip(own, "exp", 2 * k) if k else own
    rows, tall, parts = {}, {}, {}
    for k in range(chips):
        own = landed[k]
        by_x, by_y = flip(own, "rep", 1), flip(own, "rep", 2)
        if GATHER[k] == 0:
            far = (flip(by_y, "rep", 1),)
        elif GATHER[k] == 1:
            far = (flip(by_x, "rep", 2),)
        else:
            far = (flip(by_y[:capacity], "rep", 1), flip(by_x[capacity:], "rep", 2))
        rows[k] = (own, by_x, by_y, *far)
        sizes = (count, count, count, capacity, capacity) if SCATTER[k] == 2 else (count, 2 * count, count)
        *leaving, hid, pre = call(
            functools.partial(expert_kernel, len(rows[k]), SCATTER[k]),
            tuple(((n, wide), BF16) for n in sizes) + (((4 * count, units), BF16),) * 2,
            (*rows[k], w_first, w_second),
            cost_estimate=pl.CostEstimate(
                flops=8 * 4 * count * features * units, bytes_accessed=4 * features * units, transcendentals=0
            ),
        )
        tall[k], parts[k] = (hid, pre), leaving
    back = {}
    for k in range(chips):
        if SCATTER[k] == 2:
            own, to_x, to_y, via_y, via_x = parts[k]
            got_x, got_y = flip(to_x, "rep", 1), flip(to_y, "rep", 2)
            last_a = flip((f32(via_y) + f32(got_x[capacity:])).astype(BF16), "rep", 2)
            last_b = flip((f32(via_x) + f32(got_y[capacity:])).astype(BF16), "rep", 1)
            near = jnp.concatenate([got_x[:capacity], got_y[:capacity]], axis=0)
            summed = (f32(own) + f32(near) + f32(jnp.concatenate([last_a, last_b], axis=0))).astype(BF16)
        else:
            own, near, then = parts[k]
            first, second = (2, 1) if SCATTER[k] == 0 else (1, 2)
            got = flip(near, "rep", first)
            last = flip((f32(then) + f32(got[count:])).astype(BF16), "rep", second)
            summed = (f32(own) + f32(got[:count]) + f32(last)).astype(BF16)
        back[k] = flip(summed, "exp", 2 * k) if k else summed
    grads = []
    pieces = [r for k in range(chips) for r in rows[k]]
    for first in (False, True):
        args = pieces + [tall[k][1 if first else 0] for k in range(chips)]
        size = (features, units) if first else (units, features)
        tile = min(256, size[0])
        grads.append(
            pl.pallas_call(
                functools.partial(grad_kernel, len(pieces), chips, first),
                out_shape=jax.ShapeDtypeStruct(size, BF16),
                grid=(size[0] // tile,),
                in_specs=[spec] * len(args),
                out_specs=pl.BlockSpec((tile, size[1]), lambda i: (i, 0)),
                compiler_params=pltpu.CompilerParams(vmem_limit_bytes=24 << 20),
                name="grad_in" if first else "grad_out",
                cost_estimate=pl.CostEstimate(
                    flops=2 * chips * 4 * count * size[0] * size[1],
                    bytes_accessed=2 * size[0] * size[1],
                    transcendentals=0,
                ),
            )(*[vmem(a) for a in args])
        )
    other = flip(jnp.concatenate([back[k][capacity:] for k in range(chips)], axis=0), "exp", 1)
    mixed, grad_tokens = pl.pallas_call(
        functools.partial(last_kernel, capacity),
        out_shape=(jax.ShapeDtypeStruct((tok_count, features), BF16),) * 2,
        in_specs=[spec] * (6 + chips),
        out_specs=(spec,) * 2,
        compiler_params=pltpu.CompilerParams(vmem_limit_bytes=24 << 20),
        name="last",
    )(vmem(slots), tokens, gain_row, vmem(gate_columns), cotangent, *[vmem(back[k]) for k in range(chips)], vmem(other))
    return (mixed, grad_tokens, grads[1][None], grads[0][None])


def solution(mesh):
    rep, exp = mesh.shape["rep"], mesh.shape["exp"]

    def body(tokens, *rest):
        fits = rep == 4 and exp == 8 and (2 * tokens.shape[0] // exp) % 16 == 0
        return (local if fits else local_general)(tokens, *rest)

    return jax.shard_map(
        body,
        mesh=mesh,
        in_specs=(
            P(("rep", "exp"), None),
            P(),
            P(("rep", "exp"), None),
            P(("rep", "exp"), None),
            P("exp", None, "rep"),
            P("exp", "rep", None),
            P(("rep", "exp"), None),
        ),
        out_specs=(
            P(("rep", "exp"), None),
            P(("rep", "exp"), None),
            P("exp", None, "rep"),
            P("exp", "rep", None),
        ),
        check_vma=False,
    )
```

profile of v0, /device:TPU:0, one launch (start us, length us, event | category | flops | bytes accessed | tf_op | source)
XLA Modules:
  0.0 121.1 jit_solution(4505674129340788010)
XLA Ops:
  0.6 1.9 %send.1 = (bf16[128,2048]{1,0:T(8,128)(2,1)S(1)}, bf16[128,2048]{1,0:T(8,128)(2,1)S(1)}, s32[128,2]{1,0:T(8,128)S(1)}, f32[128,2]{1,0:T(8,128)S(1)}) custom-call(s32[1]{0:T(128)} %bitcast.me_ref, s32[2,128]{1,0:T(2,128)} %bitcast.20, f32[2,128]{1,0:T(2,128)} %bitcast.21, bf16[128,1024]{1,0:T(8,128)(2,1)} %tok_ref.1, f32[1,1024]{1,0:T(1,128)} %bitcast.8, ...), custom_call_target="tpu_custom_call" | custom-call | tf_op jit(solution)/shard_map/send/pallas_call | solution.py:293
  2.6 0.6 collective-permute-start
  3.2 1.5 %collective-permute-done = bf16[128,2048]{1,0:T(8,128)(2,1)S(1)} collective-permute-done((bf16[128,2048]{1,0:T(8,128)(2,1)S(1)}, bf16[128,2048]{1,0:T(8,128)(2,1)S(1)}, u32[]{:S(2)}, u32[]{:S(2)}) %collective-permute-start) | collective-permute-done | bytes 524320 | tf_op jit(solution)/shard_map/ppermute | solution.py:270
  4.7 2.9 %collective-permute-start.1 = (bf16[64,2048]{1,0:T(8,128)(2,1)S(1)}, bf16[64,2048]{1,0:T(8,128)(2,1)S(1)}, u32[]{:S(2)}, u32[]{:S(2)}) collective-permute-start(bf16[64,2048]{1,0:T(8,128)(2,1)S(1)} %pad_maximum_fusion.1.refs_0_), channel_id=1, source_target_pairs={{0,8},{8,0},{16,24},{24,16},{1,9},{9,1},{17,25},{25,17},{2,10},{10... | collective-permute-start | bytes 786440 | tf_op jit(solution)/shard_map/ppermute | solution.py:270
  7.6 1.5 %collective-permute-start.2 = (bf16[64,2048]{1,0:T(8,128)(2,1)S(1)}, bf16[64,2048]{1,0:T(8,128)(2,1)S(1)}, u32[]{:S(2)}, u32[]{:S(2)}) collective-permute-start(bf16[64,2048]{1,0:T(8,128)(2,1)S(1)} %pad_maximum_fusion.1.refs_0_), channel_id=1, source_target_pairs={{0,16},{8,24},{16,0},{24,8},{1,17},{9,25},{17,1},{25,9},{2,18},{10... | collective-permute-start | bytes 786440 | tf_op jit(solution)/shard_map/ppermute | solution.py:270
  9.2 1.6 %collective-permute-start.9 = (bf16[64,2048]{1,0:T(8,128)(2,1)S(1)}, bf16[64,2048]{1,0:T(8,128)(2,1)S(1)}, u32[]{:S(2)}, u32[]{:S(2)}) collective-permute-start(bf16[64,2048]{1,0:T(8,128)(2,1)S(1)} %pad_maximum_fusion.2), channel_id=1, source_target_pairs={{0,2},{1,3},{2,0},{3,1},{4,6},{5,7},{6,4},{7,5},{8,10},{9,11},{10,... | collective-permute-start | bytes 786440 | tf_op jit(solution)/shard_map/ppermute | solution.py:270
  10.9 2.7 %collective-permute-start.19 = (bf16[64,2048]{1,0:T(8,128)(2,1)S(1)}, bf16[64,2048]{1,0:T(8,128)(2,1)S(1)}, u32[]{:S(2)}, u32[]{:S(2)}) collective-permute-start(bf16[64,2048]{1,0:T(8,128)(2,1)S(1)} %pad_maximum_fusion.3), channel_id=1, source_target_pairs={{0,4},{1,5},{2,6},{3,7},{4,0},{5,1},{6,2},{7,3},{8,12},{9,13},{10,... | collective-permute-start | bytes 786440 | tf_op jit(solution)/shard_map/ppermute | solution.py:270
  13.5 0.3 collective-permute-start.29
  13.8 1.9 %collective-permute-done.2.refs_2_ = bf16[64,2048]{1,0:T(8,128)(2,1)S(1)} collective-permute-done((bf16[64,2048]{1,0:T(8,128)(2,1)S(1)}, bf16[64,2048]{1,0:T(8,128)(2,1)S(1)}, u32[]{:S(2)}, u32[]{:S(2)}) %collective-permute-start.2) | collective-permute-done | bytes 262176 | tf_op jit(solution)/shard_map/ppermute | solution.py:270
  15.7 0.4 collective-permute-start.3
  16.2 1.8 %collective-permute-start.4 = (bf16[32,2048]{1,0:T(8,128)(2,1)S(1)}, bf16[32,2048]{1,0:T(8,128)(2,1)S(1)}, u32[]{:S(2)}, u32[]{:S(2)}) collective-permute-start(bf16[32,2048]{1,0:T(8,128)(2,1)S(1)} %slice.146), channel_id=1, source_target_pairs={{0,16},{8,24},{16,0},{24,8},{1,17},{9,25},{17,1},{25,9},{2,18},{10... | collective-permute-start | bytes 393224 | tf_op jit(solution)/shard_map/ppermute | solution.py:270
  17.9 3.8 %collective-permute-done.9.refs_0_.refs_5_ = bf16[64,2048]{1,0:T(8,128)(2,1)S(1)} collective-permute-done((bf16[64,2048]{1,0:T(8,128)(2,1)S(1)}, bf16[64,2048]{1,0:T(8,128)(2,1)S(1)}, u32[]{:S(2)}, u32[]{:S(2)}) %collective-permute-start.9) | collective-permute-done | bytes 262176 | tf_op jit(solution)/shard_map/ppermute | solution.py:270
  21.7 0.5 collective-permute-start.10
  22.3 9.9 %collective-permute-done.19.refs_0_.refs_10_ = bf16[64,2048]{1,0:T(8,128)(2,1)S(1)} collective-permute-done((bf16[64,2048]{1,0:T(8,128)(2,1)S(1)}, bf16[64,2048]{1,0:T(8,128)(2,1)S(1)}, u32[]{:S(2)}, u32[]{:S(2)}) %collective-permute-start.19) | collective-permute-done | bytes 262176 | tf_op jit(solution)/shard_map/ppermute | solution.py:270
  32.2 0.5 collective-permute-start.11
  32.7 0.5 collective-permute-start.20
  33.3 1.5 %collective-permute-start.21 = (bf16[64,2048]{1,0:T(8,128)(2,1)S(1)}, bf16[64,2048]{1,0:T(8,128)(2,1)S(1)}, u32[]{:S(2)}, u32[]{:S(2)}) collective-permute-start(bf16[64,2048]{1,0:T(8,128)(2,1)S(1)} %collective-permute-done.19.refs_0_.refs_10_), channel_id=1, source_target_pairs={{0,16},{8,24},{16,0},{24,8},{1,17},{9,25},{17,1},{25,9},{2,18},{10... | collective-permute-start | bytes 786440 | tf_op jit(solution)/shard_map/ppermute | solution.py:270
  34.8 0.5 collective-permute-start.31
  35.3 2.6 %shard_map.102 = (bf16[64,2048]{1,0:T(8,128)(2,1)S(1)}, bf16[64,2048]{1,0:T(8,128)(2,1)S(1)}, bf16[64,2048]{1,0:T(8,128)(2,1)S(1)}, bf16[32,2048]{1,0:T(8,128)(2...) custom-call(bf16[64,2048]{1,0:T(8,128)(2,1)S(1)} %pad_maximum_fusion.1.refs_0_, ...), custom_call_target="tpu_custom_call" | custom-call | flops 2147483648 | bytes 4194304 | tf_op jit(solution)/shard_map/pallas_call | solution.py:258
  38.0 1.6 %collective-permute-start.30 = (bf16[64,2048]{1,0:T(8,128)(2,1)S(1)}, bf16[64,2048]{1,0:T(8,128)(2,1)S(1)}, u32[]{:S(2)}, u32[]{:S(2)}) collective-permute-start(bf16[64,2048]{1,0:T(8,128)(2,1)S(1)} %collective-permute-done.29.refs_0_.refs_15_), channel_id=1, source_target_pairs={{0,8},{8,0},{16,24},{24,16},{1,9},{9,1},{17,25},{25,17},{2,10},{10... | collective-permute-start | bytes 786440 | tf_op jit(solution)/shard_map/ppermute | solution.py:270
  39.5 1.9 %collective-permute-done.11.refs_2_.refs_7_ = bf16[64,2048]{1,0:T(8,128)(2,1)S(1)} collective-permute-done((bf16[64,2048]{1,0:T(8,128)(2,1)S(1)}, bf16[64,2048]{1,0:T(8,128)(2,1)S(1)}, u32[]{:S(2)}, u32[]{:S(2)}) %collective-permute-start.11) | collective-permute-done | bytes 262176 | tf_op jit(solution)/shard_map/ppermute | solution.py:270
  41.4 0.5 collective-permute-start.6
  42.0 5.1 %collective-permute-done.21.refs_2_.refs_12_ = bf16[64,2048]{1,0:T(8,128)(2,1)S(1)} collective-permute-done((bf16[64,2048]{1,0:T(8,128)(2,1)S(1)}, bf16[64,2048]{1,0:T(8,128)(2,1)S(1)}, u32[]{:S(2)}, u32[]{:S(2)}) %collective-permute-start.21) | collective-permute-done | bytes 262176 | tf_op jit(solution)/shard_map/ppermute | solution.py:270
  47.0 0.5 collective-permute-start.5
  47.6 1.6 %collective-permute-start.12 = (bf16[32,2048]{1,0:T(8,128)(2,1)S(1)}, bf16[32,2048]{1,0:T(8,128)(2,1)S(1)}, u32[]{:S(2)}, u32[]{:S(2)}) collective-permute-start(bf16[32,2048]{1,0:T(8,128)(2,1)S(1)} %slice.152), channel_id=1, source_target_pairs={{0,8},{8,0},{16,24},{24,16},{1,9},{9,1},{17,25},{25,17},{2,10},{10... | collective-permute-start | bytes 393224 | tf_op jit(solution)/shard_map/ppermute | solution.py:270
  49.2 2.5 %collective-permute-done.31.refs_2_.refs_17_ = bf16[64,2048]{1,0:T(8,128)(2,1)S(1)} collective-permute-done((bf16[64,2048]{1,0:T(8,128)(2,1)S(1)}, bf16[64,2048]{1,0:T(8,128)(2,1)S(1)}, u32[]{:S(2)}, u32[]{:S(2)}) %collective-permute-start.31) | collective-permute-done | bytes 262176 | tf_op jit(solution)/shard_map/ppermute | solution.py:270
  51.7 0.5 collective-permute-start.13
  52.2 1.5 %collective-permute-start.22 = (bf16[32,2048]{1,0:T(8,128)(2,1)S(1)}, bf16[32,2048]{1,0:T(8,128)(2,1)S(1)}, u32[]{:S(2)}, u32[]{:S(2)}) collective-permute-start(bf16[32,2048]{1,0:T(8,128)(2,1)S(1)} %slice.159), channel_id=1, source_target_pairs={{0,8},{8,0},{16,24},{24,16},{1,9},{9,1},{17,25},{25,17},{2,10},{10... | collective-permute-start | bytes 393224 | tf_op jit(solution)/shard_map/ppermute | solution.py:270
  53.8 2.2 %collective-permute-done.6 = bf16[64,2048]{1,0:T(8,128)(2,1)S(1)} collective-permute-done((bf16[64,2048]{1,0:T(8,128)(2,1)S(1)}, bf16[64,2048]{1,0:T(8,128)(2,1)S(1)}, u32[]{:S(2)}, u32[]{:S(2)}) %collective-permute-start.6) | collective-permute-done | bytes 262176 | tf_op jit(solution)/shard_map/ppermute | solution.py:270
  56.0 0.3 collective-permute-start.23
  56.4 2.2 %collective-permute-start.32 = (bf16[32,2048]{1,0:T(8,128)(2,1)S(1)}, bf16[32,2048]{1,0:T(8,128)(2,1)S(1)}, u32[]{:S(2)}, u32[]{:S(2)}) collective-permute-start(bf16[32,2048]{1,0:T(8,128)(2,1)S(1)} %slice.166), channel_id=1, source_target_pairs={{0,8},{8,0},{16,24},{24,16},{1,9},{9,1},{17,25},{25,17},{2,10},{10... | collective-permute-start | bytes 393224 | tf_op jit(solution)/shard_map/ppermute | solution.py:270
  58.6 2.1 %collective-permute-start.33 = (bf16[32,2048]{1,0:T(8,128)(2,1)S(1)}, bf16[32,2048]{1,0:T(8,128)(2,1)S(1)}, u32[]{:S(2)}, u32[]{:S(2)}) collective-permute-start(bf16[32,2048]{1,0:T(8,128)(2,1)S(1)} %slice.167), channel_id=1, source_target_pairs={{0,16},{8,24},{16,0},{24,8},{1,17},{9,25},{17,1},{25,9},{2,18},{10... | collective-permute-start | bytes 393224 | tf_op jit(solution)/shard_map/ppermute | solution.py:270
  60.7 0.5 collective-permute-start.8
  61.2 2.6 %shard_map.103 = (bf16[64,2048]{1,0:T(8,128)(2,1)S(1)}, bf16[64,2048]{1,0:T(8,128)(2,1)S(1)}, bf16[64,2048]{1,0:T(8,128)(2,1)S(1)}, bf16[32,2048]{1,0:T(8,128)(2...) custom-call(bf16[64,2048]{1,0:T(8,128)(2,1)S(1)} %collective-permute-done.9.refs, ...), custom_call_target="tpu_custom_call" | custom-call | flops 2147483648 | bytes 4194304 | tf_op jit(solution)/shard_map/pallas_call | solution.py:258
  64.0 2.0 %collective-permute-start.15 = (bf16[64,2048]{1,0:T(8,128)(2,1)S(1)}, bf16[64,2048]{1,0:T(8,128)(2,1)S(1)}, u32[]{:S(2)}, u32[]{:S(2)}) collective-permute-start(bf16[64,2048]{1,0:T(8,128)(2,1)S(1)} %get-tuple-element.49), channel_id=1, source_target_pairs={{0,16},{8,24},{16,0},{24,8},{1,17},{9,25},{17,1},{25,9},{2,18},{10... | collective-permute-start | bytes 786440 | tf_op jit(solution)/shard_map/ppermute | solution.py:270
  66.0 2.6 %shard_map.104 = (bf16[64,2048]{1,0:T(8,128)(2,1)S(1)}, bf16[64,2048]{1,0:T(8,128)(2,1)S(1)}, bf16[64,2048]{1,0:T(8,128)(2,1)S(1)}, bf16[32,2048]{1,0:T(8,128)(2...) custom-call(bf16[64,2048]{1,0:T(8,128)(2,1)S(1)} %collective-permute-done.19.ref, ...), custom_call_target="tpu_custom_call" | custom-call | flops 2147483648 | bytes 4194304 | tf_op jit(solution)/shard_map/pallas_call | solution.py:258
  68.6 1.6 %collective-permute-start.14 = (bf16[64,2048]{1,0:T(8,128)(2,1)S(1)}, bf16[64,2048]{1,0:T(8,128)(2,1)S(1)}, u32[]{:S(2)}, u32[]{:S(2)}) collective-permute-start(bf16[64,2048]{1,0:T(8,128)(2,1)S(1)} %get-tuple-element.48), channel_id=1, source_target_pairs={{0,8},{8,0},{16,24},{24,16},{1,9},{9,1},{17,25},{25,17},{2,10},{10... | collective-permute-start | bytes 786440 | tf_op jit(solution)/shard_map/ppermute | solution.py:270
  70.3 2.8 %shard_map.105 = (bf16[64,2048]{1,0:T(8,128)(2,1)S(1)}, bf16[64,2048]{1,0:T(8,128)(2,1)S(1)}, bf16[64,2048]{1,0:T(8,128)(2,1)S(1)}, bf16[32,2048]{1,0:T(8,128)(2...) custom-call(bf16[64,2048]{1,0:T(8,128)(2,1)S(1)} %collective-permute-done.29.ref, ...), custom_call_target="tpu_custom_call" | custom-call | flops 2147483648 | bytes 4194304 | tf_op jit(solution)/shard_map/pallas_call | solution.py:258
  73.1 0.9 collective-permute-done.15
  74.1 1.5 %collective-permute-start.24 = (bf16[64,2048]{1,0:T(8,128)(2,1)S(1)}, bf16[64,2048]{1,0:T(8,128)(2,1)S(1)}, u32[]{:S(2)}, u32[]{:S(2)}) collective-permute-start(bf16[64,2048]{1,0:T(8,128)(2,1)S(1)} %get-tuple-element.53), channel_id=1, source_target_pairs={{0,8},{8,0},{16,24},{24,16},{1,9},{9,1},{17,25},{25,17},{2,10},{10... | collective-permute-start | bytes 786440 | tf_op jit(solution)/shard_map/ppermute | solution.py:270
  75.6 1.6 %collective-permute-done.14 = bf16[64,2048]{1,0:T(8,128)(2,1)S(1)} collective-permute-done((bf16[64,2048]{1,0:T(8,128)(2,1)S(1)}, bf16[64,2048]{1,0:T(8,128)(2,1)S(1)}, u32[]{:S(2)}, u32[]{:S(2)}) %collective-permute-start.14) | collective-permute-done | bytes 262176 | tf_op jit(solution)/shard_map/ppermute | solution.py:270
  77.2 0.6 collective-permute-start.35
  77.9 0.9 collective-permute-done.25
  78.8 1.5 %collective-permute-start.34 = (bf16[64,2048]{1,0:T(8,128)(2,1)S(1)}, bf16[64,2048]{1,0:T(8,128)(2,1)S(1)}, u32[]{:S(2)}, u32[]{:S(2)}) collective-permute-start(bf16[64,2048]{1,0:T(8,128)(2,1)S(1)} %get-tuple-element.58), channel_id=1, source_target_pairs={{0,8},{8,0},{16,24},{24,16},{1,9},{9,1},{17,25},{25,17},{2,10},{10... | collective-permute-start | bytes 786440 | tf_op jit(solution)/shard_map/ppermute | solution.py:270
  80.3 0.7 collective-permute-done.24
  81.0 1.5 %collective-permute-start.17 = (bf16[32,2048]{1,0:T(8,128)(2,1)S(1)}, bf16[32,2048]{1,0:T(8,128)(2,1)S(1)}, u32[]{:S(2)}, u32[]{:S(2)}) collective-permute-start(bf16[32,2048]{1,0:T(8,128)(2,1)S(1)} %add_convert_fusion.8), channel_id=1, source_target_pairs={{0,8},{8,0},{16,24},{24,16},{1,9},{9,1},{17,25},{25,17},{2,10},{10... | collective-permute-start | bytes 393224 | tf_op jit(solution)/shard_map/ppermute | solution.py:270
  82.5 2.5 %collective-permute-done.35 = bf16[64,2048]{1,0:T(8,128)(2,1)S(1)} collective-permute-done((bf16[64,2048]{1,0:T(8,128)(2,1)S(1)}, bf16[64,2048]{1,0:T(8,128)(2,1)S(1)}, u32[]{:S(2)}, u32[]{:S(2)}) %collective-permute-start.35) | collective-permute-done | bytes 262176 | tf_op jit(solution)/shard_map/ppermute | solution.py:270
  85.0 0.6 collective-permute-start.16
  85.7 1.0 collective-permute-start.27
  86.9 2.1 %collective-permute-start.26 = (bf16[32,2048]{1,0:T(8,128)(2,1)S(1)}, bf16[32,2048]{1,0:T(8,128)(2,1)S(1)}, u32[]{:S(2)}, u32[]{:S(2)}) collective-permute-start(bf16[32,2048]{1,0:T(8,128)(2,1)S(1)} %add_convert_fusion.7), channel_id=1, source_target_pairs={{0,16},{8,24},{16,0},{24,8},{1,17},{9,25},{17,1},{25,9},{2,18},{10... | collective-permute-start | bytes 393224 | tf_op jit(solution)/shard_map/ppermute | solution.py:270
  88.9 1.0 collective-permute-done.16
  90.0 1.5 %collective-permute-start.37 = (bf16[32,2048]{1,0:T(8,128)(2,1)S(1)}, bf16[32,2048]{1,0:T(8,128)(2,1)S(1)}, u32[]{:S(2)}, u32[]{:S(2)}) collective-permute-start(bf16[32,2048]{1,0:T(8,128)(2,1)S(1)} %add_convert_fusion.4), channel_id=1, source_target_pairs={{0,8},{8,0},{16,24},{24,16},{1,9},{9,1},{17,25},{25,17},{2,10},{10... | collective-permute-start | bytes 393224 | tf_op jit(solution)/shard_map/ppermute | solution.py:270
  91.5 0.1 add_convert_fusion.2
  91.6 0.5 collective-permute-start.36
  92.1 3.6 %collective-permute-start.18 = (bf16[64,2048]{1,0:T(8,128)(2,1)S(1)}, bf16[64,2048]{1,0:T(8,128)(2,1)S(1)}, u32[]{:S(2)}, u32[]{:S(2)}) collective-permute-start(bf16[64,2048]{1,0:T(8,128)(2,1)S(1)} %add_convert_fusion.2), channel_id=1, source_target_pairs={{0,2},{1,3},{2,0},{3,1},{4,6},{5,7},{6,4},{7,5},{8,10},{9,11},{10,... | collective-permute-start | bytes 786440 | tf_op jit(solution)/shard_map/ppermute | solution.py:270
  95.7 0.1 add_convert_fusion.1
  95.8 2.3 %collective-permute-start.28 = (bf16[64,2048]{1,0:T(8,128)(2,1)S(1)}, bf16[64,2048]{1,0:T(8,128)(2,1)S(1)}, u32[]{:S(2)}, u32[]{:S(2)}) collective-permute-start(bf16[64,2048]{1,0:T(8,128)(2,1)S(1)} %add_convert_fusion.1), channel_id=1, source_target_pairs={{0,4},{1,5},{2,6},{3,7},{4,0},{5,1},{6,2},{7,3},{8,12},{9,13},{10,... | collective-permute-start | bytes 786440 | tf_op jit(solution)/shard_map/ppermute | solution.py:270
  98.2 1.4 %collective-permute-start.38 = (bf16[64,2048]{1,0:T(8,128)(2,1)S(1)}, bf16[64,2048]{1,0:T(8,128)(2,1)S(1)}, u32[]{:S(2)}, u32[]{:S(2)}) collective-permute-start(bf16[64,2048]{1,0:T(8,128)(2,1)S(1)} %add_convert_fusion), channel_id=1, source_target_pairs={{0,6},{1,7},{2,4},{3,5},{4,2},{5,3},{6,0},{7,1},{8,14},{9,15},{10,... | collective-permute-start | bytes 786440 | tf_op jit(solution)/shard_map/ppermute | solution.py:270
  99.6 0.1 add_convert_fusion.3.refs_0_
  99.8 8.5 %collective-permute-done.38.refs_3_ = bf16[64,2048]{1,0:T(8,128)(2,1)S(1)} collective-permute-done((bf16[64,2048]{1,0:T(8,128)(2,1)S(1)}, bf16[64,2048]{1,0:T(8,128)(2,1)S(1)}, u32[]{:S(2)}, u32[]{:S(2)}) %collective-permute-start.38) | collective-permute-done | bytes 262176 | tf_op jit(solution)/shard_map/ppermute | solution.py:270
  108.2 3.3 %collective-permute-done.28.refs_2_ = bf16[64,2048]{1,0:T(8,128)(2,1)S(1)} collective-permute-done((bf16[64,2048]{1,0:T(8,128)(2,1)S(1)}, bf16[64,2048]{1,0:T(8,128)(2,1)S(1)}, u32[]{:S(2)}, u32[]{:S(2)}) %collective-permute-start.28) | collective-permute-done | bytes 262176 | tf_op jit(solution)/shard_map/ppermute | solution.py:270
  111.7 3.9 %grad_in.1 = bf16[1024,1024]{1,0:T(8,128)(2,1)} custom-call(bf16[64,2048]{1,0:T(8,128)(2,1)S(1)} %pad_maximum_fusion.1.refs_0_, bf16[64,2048]{1,0:T(8,128)(2,1)S(1)} %collective-permute-done.1.refs_1_, bf16[64,2048]{1,0:T(8,128)(2,1)S(1)} %collective-permute-done.2.refs_2_, bf16[32,2048]{1,0:T(8,128)(2,1)S(1)} %collective-permute-done.3.refs_3_, ...), custom_call_target="tpu_custom_call" | custom-call | flops 2147483648 | bytes 2097152 | tf_op jit(solution)/shard_map/grad_in/pallas_call | solution.py:359
  115.7 3.9 %grad_out.1 = bf16[1024,1024]{1,0:T(8,128)(2,1)} custom-call(bf16[64,2048]{1,0:T(8,128)(2,1)S(1)} %pad_maximum_fusion.1.refs_0_, bf16[64,2048]{1,0:T(8,128)(2,1)S(1)} %collective-permute-done.1.refs_1_, bf16[64,2048]{1,0:T(8,128)(2,1)S(1)} %collective-permute-done.2.refs_2_, bf16[32,2048]{1,0:T(8,128)(2,1)S(1)} %collective-permute-done.3.refs_3_, ...), custom_call_target="tpu_custom_call" | custom-call | flops 2147483648 | bytes 2097152 | tf_op jit(solution)/shard_map/grad_out/pallas_call | solution.py:359
  119.6 1.5 %last.1 = (bf16[128,1024]{1,0:T(8,128)(2,1)}, bf16[128,1024]{1,0:T(8,128)(2,1)}) custom-call(s32[128,2]{1,0:T(8,128)S(1)} %get-tuple-element.38.slot_ref, bf16[128,1024]{1,0:T(8,128)(2,1)S(1)} %copy-done, f32[1,1024]{1,0:T(1,128)S(1)} %bitcast.9, f32[128,2]{1,0:T(8,128)S(1)} %get-tuple-element.39.gate_ref, bf16[128,1024]{1,0:T(8,128)(2,1)S(1)} %copy-done.1, ...), custom_call_target="tpu_custom_call" | custom-call | tf_op jit(solution)/shard_map/last/pallas_call | solution.py:375
  (79 shorter events, 1.1 us)
Async XLA Ops:
  2.6 2.1 %collective-permute-start = (bf16[128,2048]{1,0:T(8,128)(2,1)S(1)}, bf16[128,2048]{1,0:T(8,128)(2,1)S(1)}, u32[]{:S(2)}, u32[]{:S(2)}) collective-permute-start(bf16[128,2048]{1,0:T(8,128)(2,1)S(1)} %get-tuple-element.41), channel_id=1, source_target_pairs={{0,1},{1,0},{2,3},{3,2},{4,5},{5,4},{6,7},{7,6},{8,9},{9,8},{10,11... | collective-permute-start | bytes 1572872 | tf_op jit(solution)/shard_map/ppermute | solution.py:270
  3.1 32.2 %copy-start.4 = (bf16[1,1024,1024]{2,1,0:T(8,128)(2,1)S(1)}, bf16[1,1024,1024]{2,1,0:T(8,128)(2,1)}, u32[]{:S(2)}) copy-start(bf16[1,1024,1024]{2,1,0:T(8,128)(2,1)} %param.12) | copy-start | bytes 6291460
  3.2 32.1 %copy-start.3 = (bf16[1,1024,1024]{2,1,0:T(8,128)(2,1)S(1)}, bf16[1,1024,1024]{2,1,0:T(8,128)(2,1)}, u32[]{:S(2)}) copy-start(bf16[1,1024,1024]{2,1,0:T(8,128)(2,1)} %param.11) | copy-start | bytes 6291460
  4.7 11.4 %collective-permute-start.1 = (bf16[64,2048]{1,0:T(8,128)(2,1)S(1)}, bf16[64,2048]{1,0:T(8,128)(2,1)S(1)}, u32[]{:S(2)}, u32[]{:S(2)}) collective-permute-start(bf16[64,2048]{1,0:T(8,128)(2,1)S(1)} %pad_maximum_fusion.1.refs_0_), channel_id=1, source_target_pairs={{0,8},{8,0},{16,24},{24,16},{1,9},{9,1},{17,25},{25,17},{2,10},{10... | collective-permute-start | bytes 786440 | tf_op jit(solution)/shard_map/ppermute | solution.py:270
  7.6 8.1 %collective-permute-start.2 = (bf16[64,2048]{1,0:T(8,128)(2,1)S(1)}, bf16[64,2048]{1,0:T(8,128)(2,1)S(1)}, u32[]{:S(2)}, u32[]{:S(2)}) collective-permute-start(bf16[64,2048]{1,0:T(8,128)(2,1)S(1)} %pad_maximum_fusion.1.refs_0_), channel_id=1, source_target_pairs={{0,16},{8,24},{16,0},{24,8},{1,17},{9,25},{17,1},{25,9},{2,18},{10... | collective-permute-start | bytes 786440 | tf_op jit(solution)/shard_map/ppermute | solution.py:270
  9.2 12.6 %collective-permute-start.9 = (bf16[64,2048]{1,0:T(8,128)(2,1)S(1)}, bf16[64,2048]{1,0:T(8,128)(2,1)S(1)}, u32[]{:S(2)}, u32[]{:S(2)}) collective-permute-start(bf16[64,2048]{1,0:T(8,128)(2,1)S(1)} %pad_maximum_fusion.2), channel_id=1, source_target_pairs={{0,2},{1,3},{2,0},{3,1},{4,6},{5,7},{6,4},{7,5},{8,10},{9,11},{10,... | collective-permute-start | bytes 786440 | tf_op jit(solution)/shard_map/ppermute | solution.py:270
  10.9 21.4 %collective-permute-start.19 = (bf16[64,2048]{1,0:T(8,128)(2,1)S(1)}, bf16[64,2048]{1,0:T(8,128)(2,1)S(1)}, u32[]{:S(2)}, u32[]{:S(2)}) collective-permute-start(bf16[64,2048]{1,0:T(8,128)(2,1)S(1)} %pad_maximum_fusion.3), channel_id=1, source_target_pairs={{0,4},{1,5},{2,6},{3,7},{4,0},{5,1},{6,2},{7,3},{8,12},{9,13},{10,... | collective-permute-start | bytes 786440 | tf_op jit(solution)/shard_map/ppermute | solution.py:270
  13.5 19.2 %collective-permute-start.29 = (bf16[64,2048]{1,0:T(8,128)(2,1)S(1)}, bf16[64,2048]{1,0:T(8,128)(2,1)S(1)}, u32[]{:S(2)}, u32[]{:S(2)}) collective-permute-start(bf16[64,2048]{1,0:T(8,128)(2,1)S(1)} %pad_maximum_fusion.4), channel_id=1, source_target_pairs={{0,6},{1,7},{2,4},{3,5},{4,2},{5,3},{6,0},{7,1},{8,14},{9,15},{10,... | collective-permute-start | bytes 786440 | tf_op jit(solution)/shard_map/ppermute | solution.py:270
  15.7 17.6 %collective-permute-start.3 = (bf16[32,2048]{1,0:T(8,128)(2,1)S(1)}, bf16[32,2048]{1,0:T(8,128)(2,1)S(1)}, u32[]{:S(2)}, u32[]{:S(2)}) collective-permute-start(bf16[32,2048]{1,0:T(8,128)(2,1)S(1)} %slice.145), channel_id=1, source_target_pairs={{0,8},{8,0},{16,24},{24,16},{1,9},{9,1},{17,25},{25,17},{2,10},{10... | collective-permute-start | bytes 393224 | tf_op jit(solution)/shard_map/ppermute | solution.py:270
  16.2 18.6 %collective-permute-start.4 = (bf16[32,2048]{1,0:T(8,128)(2,1)S(1)}, bf16[32,2048]{1,0:T(8,128)(2,1)S(1)}, u32[]{:S(2)}, u32[]{:S(2)}) collective-permute-start(bf16[32,2048]{1,0:T(8,128)(2,1)S(1)} %slice.146), channel_id=1, source_target_pairs={{0,16},{8,24},{16,0},{24,8},{1,17},{9,25},{17,1},{25,9},{2,18},{10... | collective-permute-start | bytes 393224 | tf_op jit(solution)/shard_map/ppermute | solution.py:270
  21.7 16.2 %collective-permute-start.10 = (bf16[64,2048]{1,0:T(8,128)(2,1)S(1)}, bf16[64,2048]{1,0:T(8,128)(2,1)S(1)}, u32[]{:S(2)}, u32[]{:S(2)}) collective-permute-start(bf16[64,2048]{1,0:T(8,128)(2,1)S(1)} %collective-permute-done.9.refs_0_.refs_5_), channel_id=1, source_target_pairs={{0,8},{8,0},{16,24},{24,16},{1,9},{9,1},{17,25},{25,17},{2,10},{10... | collective-permute-start | bytes 786440 | tf_op jit(solution)/shard_map/ppermute | solution.py:270
  32.2 9.2 %collective-permute-start.11 = (bf16[64,2048]{1,0:T(8,128)(2,1)S(1)}, bf16[64,2048]{1,0:T(8,128)(2,1)S(1)}, u32[]{:S(2)}, u32[]{:S(2)}) collective-permute-start(bf16[64,2048]{1,0:T(8,128)(2,1)S(1)} %collective-permute-done.9.refs_0_.refs_5_), channel_id=1, source_target_pairs={{0,16},{8,24},{16,0},{24,8},{1,17},{9,25},{17,1},{25,9},{2,18},{10... | collective-permute-start | bytes 786440 | tf_op jit(solution)/shard_map/ppermute | solution.py:270
  32.7 14.8 %collective-permute-start.20 = (bf16[64,2048]{1,0:T(8,128)(2,1)S(1)}, bf16[64,2048]{1,0:T(8,128)(2,1)S(1)}, u32[]{:S(2)}, u32[]{:S(2)}) collective-permute-start(bf16[64,2048]{1,0:T(8,128)(2,1)S(1)} %collective-permute-done.19.refs_0_.refs_10_), channel_id=1, source_target_pairs={{0,8},{8,0},{16,24},{24,16},{1,9},{9,1},{17,25},{25,17},{2,10},{10... | collective-permute-start | bytes 786440 | tf_op jit(solution)/shard_map/ppermute | solution.py:270
  33.3 13.7 %collective-permute-start.21 = (bf16[64,2048]{1,0:T(8,128)(2,1)S(1)}, bf16[64,2048]{1,0:T(8,128)(2,1)S(1)}, u32[]{:S(2)}, u32[]{:S(2)}) collective-permute-start(bf16[64,2048]{1,0:T(8,128)(2,1)S(1)} %collective-permute-done.19.refs_0_.refs_10_), channel_id=1, source_target_pairs={{0,16},{8,24},{16,0},{24,8},{1,17},{9,25},{17,1},{25,9},{2,18},{10... | collective-permute-start | bytes 786440 | tf_op jit(solution)/shard_map/ppermute | solution.py:270
  34.8 16.9 %collective-permute-start.31 = (bf16[64,2048]{1,0:T(8,128)(2,1)S(1)}, bf16[64,2048]{1,0:T(8,128)(2,1)S(1)}, u32[]{:S(2)}, u32[]{:S(2)}) collective-permute-start(bf16[64,2048]{1,0:T(8,128)(2,1)S(1)} %collective-permute-done.29.refs_0_.refs_15_), channel_id=1, source_target_pairs={{0,16},{8,24},{16,0},{24,8},{1,17},{9,25},{17,1},{25,9},{2,18},{10... | collective-permute-start | bytes 786440 | tf_op jit(solution)/shard_map/ppermute | solution.py:270
  38.0 14.3 %collective-permute-start.30 = (bf16[64,2048]{1,0:T(8,128)(2,1)S(1)}, bf16[64,2048]{1,0:T(8,128)(2,1)S(1)}, u32[]{:S(2)}, u32[]{:S(2)}) collective-permute-start(bf16[64,2048]{1,0:T(8,128)(2,1)S(1)} %collective-permute-done.29.refs_0_.refs_15_), channel_id=1, source_target_pairs={{0,8},{8,0},{16,24},{24,16},{1,9},{9,1},{17,25},{25,17},{2,10},{10... | collective-permute-start | bytes 786440 | tf_op jit(solution)/shard_map/ppermute | solution.py:270
  41.4 14.5 %collective-permute-start.6 = (bf16[64,2048]{1,0:T(8,128)(2,1)S(1)}, bf16[64,2048]{1,0:T(8,128)(2,1)S(1)}, u32[]{:S(2)}, u32[]{:S(2)}) collective-permute-start(bf16[64,2048]{1,0:T(8,128)(2,1)S(1)} %get-tuple-element.44), channel_id=1, source_target_pairs={{0,16},{8,24},{16,0},{24,8},{1,17},{9,25},{17,1},{25,9},{2,18},{10... | collective-permute-start | bytes 786440 | tf_op jit(solution)/shard_map/ppermute | solution.py:270
  47.0 9.3 %collective-permute-start.5 = (bf16[64,2048]{1,0:T(8,128)(2,1)S(1)}, bf16[64,2048]{1,0:T(8,128)(2,1)S(1)}, u32[]{:S(2)}, u32[]{:S(2)}) collective-permute-start(bf16[64,2048]{1,0:T(8,128)(2,1)S(1)} %get-tuple-element.43), channel_id=1, source_target_pairs={{0,8},{8,0},{16,24},{24,16},{1,9},{9,1},{17,25},{25,17},{2,10},{10... | collective-permute-start | bytes 786440 | tf_op jit(solution)/shard_map/ppermute | solution.py:270
  47.6 11.0 %collective-permute-start.12 = (bf16[32,2048]{1,0:T(8,128)(2,1)S(1)}, bf16[32,2048]{1,0:T(8,128)(2,1)S(1)}, u32[]{:S(2)}, u32[]{:S(2)}) collective-permute-start(bf16[32,2048]{1,0:T(8,128)(2,1)S(1)} %slice.152), channel_id=1, source_target_pairs={{0,8},{8,0},{16,24},{24,16},{1,9},{9,1},{17,25},{25,17},{2,10},{10... | collective-permute-start | bytes 393224 | tf_op jit(solution)/shard_map/ppermute | solution.py:270
  51.7 9.0 %collective-permute-start.13 = (bf16[32,2048]{1,0:T(8,128)(2,1)S(1)}, bf16[32,2048]{1,0:T(8,128)(2,1)S(1)}, u32[]{:S(2)}, u32[]{:S(2)}) collective-permute-start(bf16[32,2048]{1,0:T(8,128)(2,1)S(1)} %slice.153), channel_id=1, source_target_pairs={{0,16},{8,24},{16,0},{24,8},{1,17},{9,25},{17,1},{25,9},{2,18},{10... | collective-permute-start | bytes 393224 | tf_op jit(solution)/shard_map/ppermute | solution.py:270
  52.2 11.6 %collective-permute-start.22 = (bf16[32,2048]{1,0:T(8,128)(2,1)S(1)}, bf16[32,2048]{1,0:T(8,128)(2,1)S(1)}, u32[]{:S(2)}, u32[]{:S(2)}) collective-permute-start(bf16[32,2048]{1,0:T(8,128)(2,1)S(1)} %slice.159), channel_id=1, source_target_pairs={{0,8},{8,0},{16,24},{24,16},{1,9},{9,1},{17,25},{25,17},{2,10},{10... | collective-permute-start | bytes 393224 | tf_op jit(solution)/shard_map/ppermute | solution.py:270
  56.0 12.7 %copy-start.5 = (bf16[64,2048]{1,0:T(8,128)(2,1)}, bf16[64,2048]{1,0:T(8,128)(2,1)S(1)}, u32[]{:S(2)}) copy-start(bf16[64,2048]{1,0:T(8,128)(2,1)S(1)} %collective-permute-done.6) | copy-start | bytes 786436
  56.0 8.0 %collective-permute-start.23 = (bf16[32,2048]{1,0:T(8,128)(2,1)S(1)}, bf16[32,2048]{1,0:T(8,128)(2,1)S(1)}, u32[]{:S(2)}, u32[]{:S(2)}) collective-permute-start(bf16[32,2048]{1,0:T(8,128)(2,1)S(1)} %slice.160), channel_id=1, source_target_pairs={{0,16},{8,24},{16,0},{24,8},{1,17},{9,25},{17,1},{25,9},{2,18},{10... | collective-permute-start | bytes 393224 | tf_op jit(solution)/shard_map/ppermute | solution.py:270
  56.4 12.3 %copy-start.6 = (bf16[64,2048]{1,0:T(8,128)(2,1)}, bf16[64,2048]{1,0:T(8,128)(2,1)S(1)}, u32[]{:S(2)}) copy-start(bf16[64,2048]{1,0:T(8,128)(2,1)S(1)} %collective-permute-done.5) | copy-start | bytes 786436
  56.4 12.3 %collective-permute-start.32 = (bf16[32,2048]{1,0:T(8,128)(2,1)S(1)}, bf16[32,2048]{1,0:T(8,128)(2,1)S(1)}, u32[]{:S(2)}, u32[]{:S(2)}) collective-permute-start(bf16[32,2048]{1,0:T(8,128)(2,1)S(1)} %slice.166), channel_id=1, source_target_pairs={{0,8},{8,0},{16,24},{24,16},{1,9},{9,1},{17,25},{25,17},{2,10},{10... | collective-permute-start | bytes 393224 | tf_op jit(solution)/shard_map/ppermute | solution.py:270
  58.6 11.6 %collective-permute-start.33 = (bf16[32,2048]{1,0:T(8,128)(2,1)S(1)}, bf16[32,2048]{1,0:T(8,128)(2,1)S(1)}, u32[]{:S(2)}, u32[]{:S(2)}) collective-permute-start(bf16[32,2048]{1,0:T(8,128)(2,1)S(1)} %slice.167), channel_id=1, source_target_pairs={{0,16},{8,24},{16,0},{24,8},{1,17},{9,25},{17,1},{25,9},{2,18},{10... | collective-permute-start | bytes 393224 | tf_op jit(solution)/shard_map/ppermute | solution.py:270
  60.7 38.9 %collective-permute-start.8 = (bf16[32,2048]{1,0:T(8,128)(2,1)S(1)}, bf16[32,2048]{1,0:T(8,128)(2,1)S(1)}, u32[]{:S(2)}, u32[]{:S(2)}) collective-permute-start(bf16[32,2048]{1,0:T(8,128)(2,1)S(1)} %add_convert_fusion.10), channel_id=1, source_target_pairs={{0,8},{8,0},{16,24},{24,16},{1,9},{9,1},{17,25},{25,17},{2,10},{10... | collective-permute-start | bytes 393224 | tf_op jit(solution)/shard_map/ppermute | solution.py:270
  63.9 35.7 %collective-permute-start.7 = (bf16[32,2048]{1,0:T(8,128)(2,1)S(1)}, bf16[32,2048]{1,0:T(8,128)(2,1)S(1)}, u32[]{:S(2)}, u32[]{:S(2)}) collective-permute-start(bf16[32,2048]{1,0:T(8,128)(2,1)S(1)} %add_convert_fusion.11), channel_id=1, source_target_pairs={{0,16},{8,24},{16,0},{24,8},{1,17},{9,25},{17,1},{25,9},{2,18},{10... | collective-permute-start | bytes 393224 | tf_op jit(solution)/shard_map/ppermute | solution.py:270
  64.0 10.1 %collective-permute-start.15 = (bf16[64,2048]{1,0:T(8,128)(2,1)S(1)}, bf16[64,2048]{1,0:T(8,128)(2,1)S(1)}, u32[]{:S(2)}, u32[]{:S(2)}) collective-permute-start(bf16[64,2048]{1,0:T(8,128)(2,1)S(1)} %get-tuple-element.49), channel_id=1, source_target_pairs={{0,16},{8,24},{16,0},{24,8},{1,17},{9,25},{17,1},{25,9},{2,18},{10... | collective-permute-start | bytes 786440 | tf_op jit(solution)/shard_map/ppermute | solution.py:270
  68.6 8.6 %collective-permute-start.14 = (bf16[64,2048]{1,0:T(8,128)(2,1)S(1)}, bf16[64,2048]{1,0:T(8,128)(2,1)S(1)}, u32[]{:S(2)}, u32[]{:S(2)}) collective-permute-start(bf16[64,2048]{1,0:T(8,128)(2,1)S(1)} %get-tuple-element.48), channel_id=1, source_target_pairs={{0,8},{8,0},{16,24},{24,16},{1,9},{9,1},{17,25},{25,17},{2,10},{10... | collective-permute-start | bytes 786440 | tf_op jit(solution)/shard_map/ppermute | solution.py:270
  70.2 8.6 %collective-permute-start.25 = (bf16[64,2048]{1,0:T(8,128)(2,1)S(1)}, bf16[64,2048]{1,0:T(8,128)(2,1)S(1)}, u32[]{:S(2)}, u32[]{:S(2)}) collective-permute-start(bf16[64,2048]{1,0:T(8,128)(2,1)S(1)} %get-tuple-element.54), channel_id=1, source_target_pairs={{0,16},{8,24},{16,0},{24,8},{1,17},{9,25},{17,1},{25,9},{2,18},{10... | collective-permute-start | bytes 786440 | tf_op jit(solution)/shard_map/ppermute | solution.py:270
  74.1 6.9 %collective-permute-start.24 = (bf16[64,2048]{1,0:T(8,128)(2,1)S(1)}, bf16[64,2048]{1,0:T(8,128)(2,1)S(1)}, u32[]{:S(2)}, u32[]{:S(2)}) collective-permute-start(bf16[64,2048]{1,0:T(8,128)(2,1)S(1)} %get-tuple-element.53), channel_id=1, source_target_pairs={{0,8},{8,0},{16,24},{24,16},{1,9},{9,1},{17,25},{25,17},{2,10},{10... | collective-permute-start | bytes 786440 | tf_op jit(solution)/shard_map/ppermute | solution.py:270
  77.2 7.8 %collective-permute-start.35 = (bf16[64,2048]{1,0:T(8,128)(2,1)S(1)}, bf16[64,2048]{1,0:T(8,128)(2,1)S(1)}, u32[]{:S(2)}, u32[]{:S(2)}) collective-permute-start(bf16[64,2048]{1,0:T(8,128)(2,1)S(1)} %get-tuple-element.59), channel_id=1, source_target_pairs={{0,16},{8,24},{16,0},{24,8},{1,17},{9,25},{17,1},{25,9},{2,18},{10... | collective-permute-start | bytes 786440 | tf_op jit(solution)/shard_map/ppermute | solution.py:270
  78.8 6.9 %collective-permute-start.34 = (bf16[64,2048]{1,0:T(8,128)(2,1)S(1)}, bf16[64,2048]{1,0:T(8,128)(2,1)S(1)}, u32[]{:S(2)}, u32[]{:S(2)}) collective-permute-start(bf16[64,2048]{1,0:T(8,128)(2,1)S(1)} %get-tuple-element.58), channel_id=1, source_target_pairs={{0,8},{8,0},{16,24},{24,16},{1,9},{9,1},{17,25},{25,17},{2,10},{10... | collective-permute-start | bytes 786440 | tf_op jit(solution)/shard_map/ppermute | solution.py:270
  81.0 5.9 %collective-permute-start.17 = (bf16[32,2048]{1,0:T(8,128)(2,1)S(1)}, bf16[32,2048]{1,0:T(8,128)(2,1)S(1)}, u32[]{:S(2)}, u32[]{:S(2)}) collective-permute-start(bf16[32,2048]{1,0:T(8,128)(2,1)S(1)} %add_convert_fusion.8), channel_id=1, source_target_pairs={{0,8},{8,0},{16,24},{24,16},{1,9},{9,1},{17,25},{25,17},{2,10},{10... | collective-permute-start | bytes 393224 | tf_op jit(solution)/shard_map/ppermute | solution.py:270
  85.0 5.0 %collective-permute-start.16 = (bf16[32,2048]{1,0:T(8,128)(2,1)S(1)}, bf16[32,2048]{1,0:T(8,128)(2,1)S(1)}, u32[]{:S(2)}, u32[]{:S(2)}) collective-permute-start(bf16[32,2048]{1,0:T(8,128)(2,1)S(1)} %add_convert_fusion.9), channel_id=1, source_target_pairs={{0,16},{8,24},{16,0},{24,8},{1,17},{9,25},{17,1},{25,9},{2,18},{10... | collective-permute-start | bytes 393224 | tf_op jit(solution)/shard_map/ppermute | solution.py:270
  85.7 6.0 %collective-permute-start.27 = (bf16[32,2048]{1,0:T(8,128)(2,1)S(1)}, bf16[32,2048]{1,0:T(8,128)(2,1)S(1)}, u32[]{:S(2)}, u32[]{:S(2)}) collective-permute-start(bf16[32,2048]{1,0:T(8,128)(2,1)S(1)} %add_convert_fusion.6), channel_id=1, source_target_pairs={{0,8},{8,0},{16,24},{24,16},{1,9},{9,1},{17,25},{25,17},{2,10},{10... | collective-permute-start | bytes 393224 | tf_op jit(solution)/shard_map/ppermute | solution.py:270
  86.8 12.9 %slice-start = ((bf16[64,2048]{1,0:T(8,128)(2,1)}), bf16[32,2048]{1,0:T(8,128)(2,1)S(1)}, s32[]{:S(2)}) async-start(bf16[64,2048]{1,0:T(8,128)(2,1)} %copy-done.5), calls=%async_computation | async-start | bytes 262144 | tf_op jit(solution)/shard_map/slice | solution.py:343
  86.8 12.9 %slice-start.1 = ((bf16[64,2048]{1,0:T(8,128)(2,1)}), bf16[32,2048]{1,0:T(8,128)(2,1)S(1)}, s32[]{:S(2)}) async-start(bf16[64,2048]{1,0:T(8,128)(2,1)} %copy-done.6), calls=%async_computation.1 | async-start | bytes 262144 | tf_op jit(solution)/shard_map/slice | solution.py:343
  86.9 5.2 %collective-permute-start.26 = (bf16[32,2048]{1,0:T(8,128)(2,1)S(1)}, bf16[32,2048]{1,0:T(8,128)(2,1)S(1)}, u32[]{:S(2)}, u32[]{:S(2)}) collective-permute-start(bf16[32,2048]{1,0:T(8,128)(2,1)S(1)} %add_convert_fusion.7), channel_id=1, source_target_pairs={{0,16},{8,24},{16,0},{24,8},{1,17},{9,25},{17,1},{25,9},{2,18},{10... | collective-permute-start | bytes 393224 | tf_op jit(solution)/shard_map/ppermute | solution.py:270
  90.0 5.8 %collective-permute-start.37 = (bf16[32,2048]{1,0:T(8,128)(2,1)S(1)}, bf16[32,2048]{1,0:T(8,128)(2,1)S(1)}, u32[]{:S(2)}, u32[]{:S(2)}) collective-permute-start(bf16[32,2048]{1,0:T(8,128)(2,1)S(1)} %add_convert_fusion.4), channel_id=1, source_target_pairs={{0,8},{8,0},{16,24},{24,16},{1,9},{9,1},{17,25},{25,17},{2,10},{10... | collective-permute-start | bytes 393224 | tf_op jit(solution)/shard_map/ppermute | solution.py:270
  91.6 6.5 %collective-permute-start.36 = (bf16[32,2048]{1,0:T(8,128)(2,1)S(1)}, bf16[32,2048]{1,0:T(8,128)(2,1)S(1)}, u32[]{:S(2)}, u32[]{:S(2)}) collective-permute-start(bf16[32,2048]{1,0:T(8,128)(2,1)S(1)} %add_convert_fusion.5), channel_id=1, source_target_pairs={{0,16},{8,24},{16,0},{24,8},{1,17},{9,25},{17,1},{25,9},{2,18},{10... | collective-permute-start | bytes 393224 | tf_op jit(solution)/shard_map/ppermute | solution.py:270
  92.1 19.5 %collective-permute-start.18 = (bf16[64,2048]{1,0:T(8,128)(2,1)S(1)}, bf16[64,2048]{1,0:T(8,128)(2,1)S(1)}, u32[]{:S(2)}, u32[]{:S(2)}) collective-permute-start(bf16[64,2048]{1,0:T(8,128)(2,1)S(1)} %add_convert_fusion.2), channel_id=1, source_target_pairs={{0,2},{1,3},{2,0},{3,1},{4,6},{5,7},{6,4},{7,5},{8,10},{9,11},{10,... | collective-permute-start | bytes 786440 | tf_op jit(solution)/shard_map/ppermute | solution.py:270
  95.8 15.8 %collective-permute-start.28 = (bf16[64,2048]{1,0:T(8,128)(2,1)S(1)}, bf16[64,2048]{1,0:T(8,128)(2,1)S(1)}, u32[]{:S(2)}, u32[]{:S(2)}) collective-permute-start(bf16[64,2048]{1,0:T(8,128)(2,1)S(1)} %add_convert_fusion.1), channel_id=1, source_target_pairs={{0,4},{1,5},{2,6},{3,7},{4,0},{5,1},{6,2},{7,3},{8,12},{9,13},{10,... | collective-permute-start | bytes 786440 | tf_op jit(solution)/shard_map/ppermute | solution.py:270
  98.2 10.0 %collective-permute-start.38 = (bf16[64,2048]{1,0:T(8,128)(2,1)S(1)}, bf16[64,2048]{1,0:T(8,128)(2,1)S(1)}, u32[]{:S(2)}, u32[]{:S(2)}) collective-permute-start(bf16[64,2048]{1,0:T(8,128)(2,1)S(1)} %add_convert_fusion), channel_id=1, source_target_pairs={{0,6},{1,7},{2,4},{3,5},{4,2},{5,3},{6,0},{7,1},{8,14},{9,15},{10,... | collective-permute-start | bytes 786440 | tf_op jit(solution)/shard_map/ppermute | solution.py:270
  111.7 7.9 %collective-permute-start.39 = (bf16[128,2048]{1,0:T(8,128)(2,1)S(1)}, bf16[128,2048]{1,0:T(8,128)(2,1)S(1)}, u32[]{:S(2)}, u32[]{:S(2)}) collective-permute-start(bf16[128,2048]{1,0:T(8,128)(2,1)S(1)} %pad_maximum_fusion), channel_id=1, source_target_pairs={{0,1},{1,0},{2,3},{3,2},{4,5},{5,4},{6,7},{7,6},{8,9},{9,8},{10,11... | collective-permute-start | bytes 1572872 | tf_op jit(solution)/shard_map/ppermute | solution.py:270
  115.7 3.9 %copy-start = (bf16[128,1024]{1,0:T(8,128)(2,1)S(1)}, bf16[128,1024]{1,0:T(8,128)(2,1)}, u32[]{:S(2)}) copy-start(bf16[128,1024]{1,0:T(8,128)(2,1)} %tok_ref.1) | copy-start | bytes 786436
  115.7 3.9 %copy-start.1 = (bf16[128,1024]{1,0:T(8,128)(2,1)S(1)}, bf16[128,1024]{1,0:T(8,128)(2,1)}, u32[]{:S(2)}) copy-start(bf16[128,1024]{1,0:T(8,128)(2,1)} %cot_ref.1) | copy-start | bytes 786436
  115.7 3.9 %copy-start.2 = (f32[1024]{0:T(1024)S(1)}, f32[1024]{0:T(1024)}, u32[]{:S(2)}) copy-start(f32[1024]{0:T(1024)} %param.8) | copy-start | bytes 12292
where the time goes:
time: 123 us; the launch traced here: 121 us
  starting transfers between devices  48.6 us (40%)
  waiting for transfers between devices  48.3 us (39%)
  Pallas kernels  22 us (18%)
    ppermute x40, starting transfers between devices, flip(): return lax.ppermute(array, axis_name, [(i, i ^ mask) for i in range(size)])  48.6 us
    ppermute x40, waiting for transfers between devices, flip(): return lax.ppermute(array, axis_name, [(i, i ^ mask) for i in range(size)])  48.3 us
    pallas_call x4, Pallas kernels, call(): pl.pallas_call(kernel, out_shape=tuple((pltpu.VMEM(s, d) for s, d in outs...  10.7 us
    pallas_call x2, Pallas kernels, local_inner(): pl.pallas_call(functools.partial(grad_kernel, len(pieces), chips, first),...  7.85 us
  transfers between devices with their start and end apart: 40, of which 16 were waited for; matrix products, arithmetic and copies ran while one was open for 1% of the time, Pallas kernels for 15%

commit v1 on v0

--- a/solution.py
+++ b/solution.py
@@ -13,7 +13,7 @@
 CUBIC = 0.044715
 BF16, F32 = jnp.bfloat16, jnp.float32
 GATHER = (2, 2, 2, 2)
-SCATTER = (2, 2, 2, 2)
+SCATTER = (3, 2, 3, 2)
 
 
 def normalize(entries, gain):
@@ -190,7 +190,18 @@
         pre_ref[:, at] = (dh * slope).astype(BF16)
     hid, pre = hid_ref[...], pre_ref[...]
     half = count // 2
-    if form == 2:
+    if form == 3:
+        moves = (
+            (0, 0, half, 0, 0),
+            (1, 0, half, 1, 0),
+            (3, 0, half, 1, half),
+            (2, 0, half, 2, 0),
+            (2, half, count, 3, 0),
+            (3, half, count, 3, half),
+            (1, half, count, 3, count),
+            (0, half, count, 3, count + half),
+        )
+    elif form == 2:
         moves = (
             (0, 0, count, 0, 0),
             (1, 0, half, 1, 0),
@@ -212,9 +223,11 @@
             outs[out][there, features + j : features + j + tile] = dx[rows]
 
 
-def grad_kernel(pieces, chips, first, *refs):
+def grad_kernel(pieces, chips, first, base, *refs):
+    if base:
+        refs = refs[1:]
     rows, tall, out_ref = refs[:pieces], refs[pieces : pieces + chips], refs[pieces + chips]
-    step = pl.program_id(0)
+    step = pl.program_id(0) + base
     tile = out_ref.shape[0]
     features = rows[0].shape[1] // 2
     at = pl.ds(pl.multiple_of(step * tile, tile), tile)
@@ -227,11 +240,13 @@
     out_ref[...] = dot_tn(left, right).astype(BF16)
 
 
-def last_kernel(capacity, slot_ref, tok_ref, gain_ref, gate_ref, cot_ref, *refs):
-    pieces, other_ref, mixed_ref, grad_ref = refs[:-3], refs[-3], refs[-2], refs[-1]
+def last_kernel(capacity, chips, late, slot_ref, tok_ref, gain_ref, gate_ref, cot_ref, *refs):
+    pieces, mixed_ref, grad_ref = refs[:-2], refs[-2], refs[-1]
     count, features = tok_ref.shape
-    own = jnp.concatenate([p[:capacity] for p in pieces], axis=0)
-    returned = jnp.concatenate([own, other_ref[...]], axis=0)
+    odd = [pieces[k][capacity:] for k in range(chips)]
+    for i, k in enumerate(late):
+        odd[k] = pieces[chips][i * capacity : (i + 1) * capacity]
+    returned = jnp.concatenate([p[:capacity] for p in pieces[:chips]] + odd, axis=0)
     lane = lax.broadcasted_iota(jnp.int32, (count, returned.shape[0]), 1)
     picks = [(slot_ref[:, k : k + 1] == lane).astype(F32) for k in range(2)]
     values = tok_ref[...].astype(F32)
@@ -323,7 +338,10 @@
         else:
             far = (flip(by_y[:capacity], "rep", 1), flip(by_x[capacity:], "rep", 2))
         rows[k] = (own, by_x, by_y, *far)
-        sizes = (count, count, count, capacity, capacity) if SCATTER[k] == 2 else (count, 2 * count, count)
+        if SCATTER[k] == 3:
+            sizes = (capacity, count, capacity, 2 * count)
+        else:
+            sizes = (count, count, count, capacity, capacity) if SCATTER[k] == 2 else (count, 2 * count, count)
         *leaving, hid, pre = call(
             functools.partial(expert_kernel, len(rows[k]), SCATTER[k]),
             tuple(((n, wide), BF16) for n in sizes) + (((4 * count, units), BF16),) * 2,
@@ -335,11 +353,19 @@
         tall[k], parts[k] = (hid, pre), leaving
     back = {}
     for k in range(chips):
-        if SCATTER[k] == 2:
-            own, to_x, to_y, via_y, via_x = parts[k]
+        if SCATTER[k] >= 2:
+            if SCATTER[k] == 3:
+                own, to_x, via_y, swap_k = parts[k]
+                swap_k = flip(swap_k, "exp", 1)
+                to_y = swap_k[:count]
+                via_x = swap_k[count : count + capacity]
+                own = jnp.concatenate([own, swap_k[count + capacity :]], axis=0)
+            else:
+                own, to_x, to_y, via_y, via_x = parts[k]
             got_x, got_y = flip(to_x, "rep", 1), flip(to_y, "rep", 2)
-            last_a = flip((f32(via_y) + f32(got_x[capacity:])).astype(BF16), "rep", 2)
-            last_b = flip((f32(via_x) + f32(got_y[capacity:])).astype(BF16), "rep", 1)
+            sum_a = (f32(via_y) + f32(got_x[capacity:])).astype(BF16)
+            sum_b = (f32(via_x) + f32(got_y[capacity:])).astype(BF16)
+            last_a, last_b = flip(sum_a, "rep", 2), flip(sum_b, "rep", 1)
             near = jnp.concatenate([got_x[:capacity], got_y[:capacity]], axis=0)
             summed = (f32(own) + f32(near) + f32(jnp.concatenate([last_a, last_b], axis=0))).astype(BF16)
         else:
@@ -352,34 +378,48 @@
     grads = []
     pieces = [r for k in range(chips) for r in rows[k]]
     for first in (False, True):
-        args = pieces + [tall[k][1 if first else 0] for k in range(chips)]
+        args = [vmem(a) for a in pieces + [tall[k][1 if first else 0] for k in range(chips)]]
         size = (features, units) if first else (units, features)
         tile = min(256, size[0])
-        grads.append(
-            pl.pallas_call(
-                functools.partial(grad_kernel, len(pieces), chips, first),
+        steps = size[0] // tile
+        done = None
+        for base in (0, steps // 2):
+            done = pl.pallas_call(
+                functools.partial(grad_kernel, len(pieces), chips, first, base),
                 out_shape=jax.ShapeDtypeStruct(size, BF16),
-                grid=(size[0] // tile,),
-                in_specs=[spec] * len(args),
-                out_specs=pl.BlockSpec((tile, size[1]), lambda i: (i, 0)),
+                grid=(steps - base if base else steps // 2,),
+                in_specs=([pl.BlockSpec(memory_space=pl.ANY)] if base else []) + [spec] * len(args),
+                out_specs=pl.BlockSpec((tile, size[1]), lambda i, base=base: (i + base, 0)),
+                input_output_aliases={0: 0} if base else {},
                 compiler_params=pltpu.CompilerParams(vmem_limit_bytes=24 << 20),
                 name="grad_in" if first else "grad_out",
                 cost_estimate=pl.CostEstimate(
-                    flops=2 * chips * 4 * count * size[0] * size[1],
-                    bytes_accessed=2 * size[0] * size[1],
+                    flops=chips * 4 * count * size[0] * size[1],
+                    bytes_accessed=size[0] * size[1],
                     transcendentals=0,
                 ),
-            )(*[vmem(a) for a in args])
-        )
-    other = flip(jnp.concatenate([back[k][capacity:] for k in range(chips)], axis=0), "exp", 1)
+            )(*([done] if base else []), *args)
+        grads.append(done)
+    late = [k for k in range(chips) if SCATTER[k] != 3]
+    other = flip(jnp.concatenate([back[k][capacity:] for k in late], axis=0), "exp", 1) if late else None
+    ready = [vmem(back[k]) for k in range(chips)]
+    if late:
+        ready.append(vmem(other))
     mixed, grad_tokens = pl.pallas_call(
-        functools.partial(last_kernel, capacity),
+        functools.partial(last_kernel, capacity, chips, late),
         out_shape=(jax.ShapeDtypeStruct((tok_count, features), BF16),) * 2,
-        in_specs=[spec] * (6 + chips),
+        in_specs=[spec] * (5 + len(ready)),
         out_specs=(spec,) * 2,
         compiler_params=pltpu.CompilerParams(vmem_limit_bytes=24 << 20),
         name="last",
-    )(vmem(slots), tokens, gain_row, vmem(gate_columns), cotangent, *[vmem(back[k]) for k in range(chips)], vmem(other))
+    )(
+        vmem(slots),
+        tokens,
+        gain_row,
+        vmem(gate_columns),
+        cotangent,
+        *ready,
+    )
     return (mixed, grad_tokens, grads[1][None], grads[0][None])
 
 

time: 123 us -> 138 us (1.12); the launches traced: 121 us -> 138 us
  waiting for transfers between devices: 48.3 us -> 67.7 us
  starting transfers between devices: 48.6 us -> 44.4 us
  Pallas kernels: 22 us -> 23.5 us
    ppermute x40 -> x42, waiting for transfers between devices: 48.3 us -> 67.7 us  [flip(): return lax.ppermute(array, axis_name, [(i, i ^ mask) for i in range(size)])]
    ppermute x40 -> x42, starting transfers between devices: 48.6 us -> 44.4 us  [flip(): return lax.ppermute(array, axis_name, [(i, i ^ mask) for i in range(size)])]
    pallas_call x3 -> x5, Pallas kernels: 9.33 us -> 10.9 us  [the longest x4 9.37 us: local_inner(): pl.pallas_call(functools.partial(grad_kernel, len(pieces), chips, first,...]
  transfers between devices with their start and end apart: 40 -> 42, of which waited for: 16 -> 17; matrix products, arithmetic and copies ran while one was open for 1% -> 1% of each run, Pallas kernels for 15% -> 15%
where the time goes in v1:
time: 138 us
  waiting for transfers between devices  67.7 us (49%)
  starting transfers between devices  44.4 us (32%)
  Pallas kernels  23.5 us (17%)
    ppermute x42, waiting for transfers between devices, flip(): return lax.ppermute(array, axis_name, [(i, i ^ mask) for i in range(size)])  67.7 us
    ppermute x42, starting transfers between devices, flip(): return lax.ppermute(array, axis_name, [(i, i ^ mask) for i in range(size)])  44.4 us
    pallas_call x4, Pallas kernels, call(): pl.pallas_call(kernel, out_shape=tuple((pltpu.VMEM(s, d) for s, d in outs...  10.7 us
    pallas_call x4, Pallas kernels, local_inner(): pl.pallas_call(functools.partial(grad_kernel, len(pieces), chips, first,...  9.37 us
  transfers between devices with their start and end apart: 42, of which 17 were waited for; matrix products, arithmetic and copies ran while one was open for 1% of the time, Pallas kernels for 15%

profile of v1, /device:TPU:0, one launch (start us, length us, event | category | flops | bytes accessed | tf_op | source)
XLA Modules:
  0.0 137.8 jit_solution(13572900664077244077)
XLA Ops:
  0.6 1.9 %send.1 = (bf16[128,2048]{1,0:T(8,128)(2,1)S(1)}, bf16[128,2048]{1,0:T(8,128)(2,1)S(1)}, s32[128,2]{1,0:T(8,128)S(1)}, f32[128,2]{1,0:T(8,128)S(1)}) custom-call(s32[1]{0:T(128)} %bitcast.me_ref, s32[2,128]{1,0:T(2,128)} %bitcast.20, f32[2,128]{1,0:T(2,128)} %bitcast.21, bf16[128,1024]{1,0:T(8,128)(2,1)} %tok_ref.1, f32[1,1024]{1,0:T(1,128)} %bitcast.8, ...), custom_call_target="tpu_custom_call" | custom-call | tf_op jit(solution)/shard_map/send/pallas_call | solution.py:308
  2.6 0.6 collective-permute-start
  3.2 1.5 %collective-permute-done = bf16[128,2048]{1,0:T(8,128)(2,1)S(1)} collective-permute-done((bf16[128,2048]{1,0:T(8,128)(2,1)S(1)}, bf16[128,2048]{1,0:T(8,128)(2,1)S(1)}, u32[]{:S(2)}, u32[]{:S(2)}) %collective-permute-start) | collective-permute-done | bytes 524320 | tf_op jit(solution)/shard_map/ppermute | solution.py:285
  4.7 2.9 %collective-permute-start.2 = (bf16[64,2048]{1,0:T(8,128)(2,1)S(1)}, bf16[64,2048]{1,0:T(8,128)(2,1)S(1)}, u32[]{:S(2)}, u32[]{:S(2)}) collective-permute-start(bf16[64,2048]{1,0:T(8,128)(2,1)S(1)} %pad_maximum_fusion.refs_0_.refs_1_), channel_id=1, source_target_pairs={{0,16},{8,24},{16,0},{24,8},{1,17},{9,25},{17,1},{25,9},{2,18},{10... | collective-permute-start | bytes 786440 | tf_op jit(solution)/shard_map/ppermute | solution.py:285
  7.7 1.5 %collective-permute-start.1 = (bf16[64,2048]{1,0:T(8,128)(2,1)S(1)}, bf16[64,2048]{1,0:T(8,128)(2,1)S(1)}, u32[]{:S(2)}, u32[]{:S(2)}) collective-permute-start(bf16[64,2048]{1,0:T(8,128)(2,1)S(1)} %pad_maximum_fusion.refs_0_.refs_1_), channel_id=1, source_target_pairs={{0,8},{8,0},{16,24},{24,16},{1,9},{9,1},{17,25},{25,17},{2,10},{10... | collective-permute-start | bytes 786440 | tf_op jit(solution)/shard_map/ppermute | solution.py:285
  9.2 1.6 %collective-permute-start.10 = (bf16[64,2048]{1,0:T(8,128)(2,1)S(1)}, bf16[64,2048]{1,0:T(8,128)(2,1)S(1)}, u32[]{:S(2)}, u32[]{:S(2)}) collective-permute-start(bf16[64,2048]{1,0:T(8,128)(2,1)S(1)} %pad_maximum_fusion.1), channel_id=1, source_target_pairs={{0,2},{1,3},{2,0},{3,1},{4,6},{5,7},{6,4},{7,5},{8,10},{9,11},{10,... | collective-permute-start | bytes 786440 | tf_op jit(solution)/shard_map/ppermute | solution.py:285
  10.9 2.7 %collective-permute-start.20 = (bf16[64,2048]{1,0:T(8,128)(2,1)S(1)}, bf16[64,2048]{1,0:T(8,128)(2,1)S(1)}, u32[]{:S(2)}, u32[]{:S(2)}) collective-permute-start(bf16[64,2048]{1,0:T(8,128)(2,1)S(1)} %pad_maximum_fusion.2), channel_id=1, source_target_pairs={{0,4},{1,5},{2,6},{3,7},{4,0},{5,1},{6,2},{7,3},{8,12},{9,13},{10,... | collective-permute-start | bytes 786440 | tf_op jit(solution)/shard_map/ppermute | solution.py:285
  13.5 0.3 collective-permute-start.31
  13.8 0.5 collective-permute-done.2.refs_2_.refs_3_
  14.3 1.8 %collective-permute-start.3 = (bf16[32,2048]{1,0:T(8,128)(2,1)S(1)}, bf16[32,2048]{1,0:T(8,128)(2,1)S(1)}, u32[]{:S(2)}, u32[]{:S(2)}) collective-permute-start(bf16[32,2048]{1,0:T(8,128)(2,1)S(1)} %slice.161), channel_id=1, source_target_pairs={{0,8},{8,0},{16,24},{24,16},{1,9},{9,1},{17,25},{25,17},{2,10},{10... | collective-permute-start | bytes 393224 | tf_op jit(solution)/shard_map/ppermute | solution.py:285
  16.1 1.6 %collective-permute-start.4 = (bf16[32,2048]{1,0:T(8,128)(2,1)S(1)}, bf16[32,2048]{1,0:T(8,128)(2,1)S(1)}, u32[]{:S(2)}, u32[]{:S(2)}) collective-permute-start(bf16[32,2048]{1,0:T(8,128)(2,1)S(1)} %slice.162), channel_id=1, source_target_pairs={{0,16},{8,24},{16,0},{24,8},{1,17},{9,25},{17,1},{25,9},{2,18},{10... | collective-permute-start | bytes 393224 | tf_op jit(solution)/shard_map/ppermute | solution.py:285
  17.7 4.1 %collective-permute-done.10.refs_0_.refs_5_.refs_6_ = bf16[64,2048]{1,0:T(8,128)(2,1)S(1)} collective-permute-done((bf16[64,2048]{1,0:T(8,128)(2,1)S(1)}, bf16[64,2048]{1,0:T(8,128)(2,1)S(1)}, u32[]{:S(2)}, u32[]{:S(2)}) %collective-permute-start.10) | collective-permute-done | bytes 262176 | tf_op jit(solution)/shard_map/ppermute | solution.py:285
  21.7 0.5 collective-permute-start.12
  22.3 10.0 %collective-permute-done.20.refs_0_.refs_10_.refs_11_ = bf16[64,2048]{1,0:T(8,128)(2,1)S(1)} collective-permute-done((bf16[64,2048]{1,0:T(8,128)(2,1)S(1)}, bf16[64,2048]{1,0:T(8,128)(2,1)S(1)}, u32[]{:S(2)}, u32[]{:S(2)}) %collective-permute-start.20) | collective-permute-done | bytes 262176 | tf_op jit(solution)/shard_map/ppermute | solution.py:285
  32.2 0.5 collective-permute-start.11
  32.8 0.5 collective-permute-start.22
  33.3 1.5 %collective-permute-start.21 = (bf16[64,2048]{1,0:T(8,128)(2,1)S(1)}, bf16[64,2048]{1,0:T(8,128)(2,1)S(1)}, u32[]{:S(2)}, u32[]{:S(2)}) collective-permute-start(bf16[64,2048]{1,0:T(8,128)(2,1)S(1)} %collective-permute-done.20.refs_0_.refs_10_.refs_11_), channel_id=1, source_target_pairs={{0,8},{8,0},{16,24},{24,16},{1,9},{9,1},{17,25},{25,17},{2,10},{10... | collective-permute-start | bytes 786440 | tf_op jit(solution)/shard_map/ppermute | solution.py:285
  34.8 1.5 %collective-permute-start.33 = (bf16[64,2048]{1,0:T(8,128)(2,1)S(1)}, bf16[64,2048]{1,0:T(8,128)(2,1)S(1)}, u32[]{:S(2)}, u32[]{:S(2)}) collective-permute-start(bf16[64,2048]{1,0:T(8,128)(2,1)S(1)} %collective-permute-done.31.refs_0_.refs_15_.refs_16_), channel_id=1, source_target_pairs={{0,16},{8,24},{16,0},{24,8},{1,17},{9,25},{17,1},{25,9},{2,18},{10... | collective-permute-start | bytes 786440 | tf_op jit(solution)/shard_map/ppermute | solution.py:285
  36.3 2.6 %shard_map.102 = (bf16[32,2048]{1,0:T(8,128)(2,1)S(1)}, bf16[64,2048]{1,0:T(8,128)(2,1)S(1)}, bf16[32,2048]{1,0:T(8,128)(2,1)S(1)}, bf16[128,2048]{1,0:T(8,128)(...) custom-call(bf16[64,2048]{1,0:T(8,128)(2,1)S(1)} %pad_maximum_fusion.refs_0_.refs_1_, ...), custom_call_target="tpu_custom_call" | custom-call | flops 2147483648 | bytes 4194304 | tf_op jit(solution)/shard_map/pallas_call | solution.py:273
  39.0 0.6 collective-permute-start.32
  39.6 1.5 %collective-permute-done.11.refs_1_.refs_6_.refs_7_ = bf16[64,2048]{1,0:T(8,128)(2,1)S(1)} collective-permute-done((bf16[64,2048]{1,0:T(8,128)(2,1)S(1)}, bf16[64,2048]{1,0:T(8,128)(2,1)S(1)}, u32[]{:S(2)}, u32[]{:S(2)}) %collective-permute-start.11) | collective-permute-done | bytes 262176 | tf_op jit(solution)/shard_map/ppermute | solution.py:285
  41.2 5.5 %collective-permute-done.21.refs_1_.refs_11_.refs_12_ = bf16[64,2048]{1,0:T(8,128)(2,1)S(1)} collective-permute-done((bf16[64,2048]{1,0:T(8,128)(2,1)S(1)}, bf16[64,2048]{1,0:T(8,128)(2,1)S(1)}, u32[]{:S(2)}, u32[]{:S(2)}) %collective-permute-start.21) | collective-permute-done | bytes 262176 | tf_op jit(solution)/shard_map/ppermute | solution.py:285
  46.7 0.6 collective-permute-start.14
  47.3 5.0 %collective-permute-done.32.refs_1_.refs_16_.refs_17_ = bf16[64,2048]{1,0:T(8,128)(2,1)S(1)} collective-permute-done((bf16[64,2048]{1,0:T(8,128)(2,1)S(1)}, bf16[64,2048]{1,0:T(8,128)(2,1)S(1)}, u32[]{:S(2)}, u32[]{:S(2)}) %collective-permute-start.32) | collective-permute-done | bytes 262176 | tf_op jit(solution)/shard_map/ppermute | solution.py:285
  52.3 3.1 %collective-permute-done.6 = bf16[64,2048]{1,0:T(8,128)(2,1)S(1)} collective-permute-done((bf16[64,2048]{1,0:T(8,128)(2,1)S(1)}, bf16[64,2048]{1,0:T(8,128)(2,1)S(1)}, u32[]{:S(2)}, u32[]{:S(2)}) %collective-permute-start.6) | collective-permute-done | bytes 262176 | tf_op jit(solution)/shard_map/ppermute | solution.py:285
  55.5 0.5 collective-permute-start.35
  56.0 3.7 %collective-permute-done.34.refs_3_.refs_18_.refs_19_ = bf16[32,2048]{1,0:T(8,128)(2,1)S(1)} collective-permute-done((bf16[32,2048]{1,0:T(8,128)(2,1)S(1)}, bf16[32,2048]{1,0:T(8,128)(2,1)S(1)}, u32[]{:S(2)}, u32[]{:S(2)}) %collective-permute-start.34) | collective-permute-done | bytes 131104 | tf_op jit(solution)/shard_map/ppermute | solution.py:285
  59.7 0.5 collective-permute-start.23
  60.2 0.5 collective-permute-done.35.refs_4_.refs_19_.refs_20_
  60.8 0.2 collective-permute-start.24
  60.9 2.6 %shard_map.105 = (bf16[64,2048]{1,0:T(8,128)(2,1)S(1)}, bf16[64,2048]{1,0:T(8,128)(2,1)S(1)}, bf16[64,2048]{1,0:T(8,128)(2,1)S(1)}, bf16[32,2048]{1,0:T(8,128)(2...) custom-call(bf16[64,2048]{1,0:T(8,128)(2,1)S(1)} %collective-permute-done.31.ref, ...), custom_call_target="tpu_custom_call" | custom-call | flops 2147483648 | bytes 4194304 | tf_op jit(solution)/shard_map/pallas_call | solution.py:273
  63.6 1.3 collective-permute-start.36
  64.9 1.5 %collective-permute-start.37 = (bf16[64,2048]{1,0:T(8,128)(2,1)S(1)}, bf16[64,2048]{1,0:T(8,128)(2,1)S(1)}, u32[]{:S(2)}, u32[]{:S(2)}) collective-permute-start(bf16[64,2048]{1,0:T(8,128)(2,1)S(1)} %get-tuple-element.55), channel_id=1, source_target_pairs={{0,16},{8,24},{16,0},{24,8},{1,17},{9,25},{17,1},{25,9},{2,18},{10... | collective-permute-start | bytes 786440 | tf_op jit(solution)/shard_map/ppermute | solution.py:285
  66.4 2.6 %shard_map.103 = (bf16[64,2048]{1,0:T(8,128)(2,1)S(1)}, bf16[64,2048]{1,0:T(8,128)(2,1)S(1)}, bf16[64,2048]{1,0:T(8,128)(2,1)S(1)}, bf16[32,2048]{1,0:T(8,128)(2...) custom-call(bf16[64,2048]{1,0:T(8,128)(2,1)S(1)} %collective-permute-done.10.ref, ...), custom_call_target="tpu_custom_call" | custom-call | flops 2147483648 | bytes 4194304 | tf_op jit(solution)/shard_map/pallas_call | solution.py:273
  69.1 1.2 collective-permute-start.15
  70.3 0.2 collective-permute-start.16
  70.4 2.8 %shard_map.104 = (bf16[32,2048]{1,0:T(8,128)(2,1)S(1)}, bf16[64,2048]{1,0:T(8,128)(2,1)S(1)}, bf16[32,2048]{1,0:T(8,128)(2,1)S(1)}, bf16[128,2048]{1,0:T(8,128)(...) custom-call(bf16[64,2048]{1,0:T(8,128)(2,1)S(1)} %collective-permute-done.20.refs_0_.refs_10_.refs_11_, ...), custom_call_target="tpu_custom_call" | custom-call | flops 2147483648 | bytes 4194304 | tf_op jit(solution)/shard_map/pallas_call | solution.py:273
  73.3 2.4 %grad_in.2.refs_0_ = bf16[1024,1024]{1,0:T(8,128)(2,1)} custom-call(bf16[64,2048]{1,0:T(8,128)(2,1)S(1)} %pad_maximum_fusion.refs_0_.refs_1_, bf16[64,2048]{1,0:T(8,128)(2,1)S(1)} %collective-permute-done.1.refs_1_.refs_2_, bf16[64,2048]{1,0:T(8,128)(2,1)S(1)} %collective-permute-done.2.refs_2_.refs_3_, ...), custom_call_target="tpu_custom_call" | custom-call | flops 1073741824 | bytes 1048576 | tf_op jit(solution)/shard_map/grad_in/pallas_call | solution.py:387
  75.6 2.3 %grad_in.3 = bf16[1024,1024]{1,0:T(8,128)(2,1)} custom-call(bf16[1024,1024]{1,0:T(8,128)(2,1)} %grad_in.2.refs_0_, bf16[64,2048]{1,0:T(8,128)(2,1)S(1)} %pad_maximum_fusion.refs_0_.refs_1_, bf16[64,2048]{1,0:T(8,128)(2,1)S(1)} %collective-permute-done.1.refs_1_.refs_2_, ...), custom_call_target="tpu_custom_call", output_to_operand_aliasing={{}: (0, {})} | custom-call | flops 1073741824 | bytes 1048576 | tf_op jit(solution)/shard_map/grad_in/pallas_call | solution.py:387
  78.0 2.3 %grad_out.2.refs_0_ = bf16[1024,1024]{1,0:T(8,128)(2,1)} custom-call(bf16[64,2048]{1,0:T(8,128)(2,1)S(1)} %pad_maximum_fusion.refs_0_.refs_1_, bf16[64,2048]{1,0:T(8,128)(2,1)S(1)} %collective-permute-done.1.refs_1_.refs_2_, bf16[64,2048]{1,0:T(8,128)(2,1)S(1)} %collective-permute-done.2.refs_2_.refs_3_, ...), custom_call_target="tpu_custom_call" | custom-call | flops 1073741824 | bytes 1048576 | tf_op jit(solution)/shard_map/grad_out/pallas_call | solution.py:387
  80.3 1.8 %collective-permute-start.8 = (bf16[32,2048]{1,0:T(8,128)(2,1)S(1)}, bf16[32,2048]{1,0:T(8,128)(2,1)S(1)}, u32[]{:S(2)}, u32[]{:S(2)}) collective-permute-start(bf16[32,2048]{1,0:T(8,128)(2,1)S(1)} %add_convert_fusion.11), channel_id=1, source_target_pairs={{0,16},{8,24},{16,0},{24,8},{1,17},{9,25},{17,1},{25,9},{2,18},{10... | collective-permute-start | bytes 393224 | tf_op jit(solution)/shard_map/ppermute | solution.py:285
  82.2 1.0 collective-permute-start.26
  83.4 0.6 collective-permute-start.7
  84.0 1.6 %collective-permute-start.38 = (bf16[32,2048]{1,0:T(8,128)(2,1)S(1)}, bf16[32,2048]{1,0:T(8,128)(2,1)S(1)}, u32[]{:S(2)}, u32[]{:S(2)}) collective-permute-start(bf16[32,2048]{1,0:T(8,128)(2,1)S(1)} %add_convert_fusion.5), channel_id=1, source_target_pairs={{0,16},{8,24},{16,0},{24,8},{1,17},{9,25},{17,1},{25,9},{2,18},{10... | collective-permute-start | bytes 393224 | tf_op jit(solution)/shard_map/ppermute | solution.py:285
  85.6 3.4 %collective-permute-done.26 = bf16[64,2048]{1,0:T(8,128)(2,1)S(1)} collective-permute-done((bf16[64,2048]{1,0:T(8,128)(2,1)S(1)}, bf16[64,2048]{1,0:T(8,128)(2,1)S(1)}, u32[]{:S(2)}, u32[]{:S(2)}) %collective-permute-start.26) | collective-permute-done | bytes 262176 | tf_op jit(solution)/shard_map/ppermute | solution.py:285
  89.0 0.8 collective-permute-start.39
  89.9 5.0 %collective-permute-done.38 = bf16[32,2048]{1,0:T(8,128)(2,1)S(1)} collective-permute-done((bf16[32,2048]{1,0:T(8,128)(2,1)S(1)}, bf16[32,2048]{1,0:T(8,128)(2,1)S(1)}, u32[]{:S(2)}, u32[]{:S(2)}) %collective-permute-start.38) | collective-permute-done | bytes 131104 | tf_op jit(solution)/shard_map/ppermute | solution.py:285
  94.9 0.6 collective-permute-start.17
  95.5 0.9 collective-permute-start.18
  96.6 3.4 %collective-permute-done.17 = bf16[32,2048]{1,0:T(8,128)(2,1)S(1)} collective-permute-done((bf16[32,2048]{1,0:T(8,128)(2,1)S(1)}, bf16[32,2048]{1,0:T(8,128)(2,1)S(1)}, u32[]{:S(2)}, u32[]{:S(2)}) %collective-permute-start.17) | collective-permute-done | bytes 131104 | tf_op jit(solution)/shard_map/ppermute | solution.py:285
  100.0 0.7 collective-permute-start.28
  100.7 3.0 %collective-permute-start.40 = (bf16[64,2048]{1,0:T(8,128)(2,1)S(1)}, bf16[64,2048]{1,0:T(8,128)(2,1)S(1)}, u32[]{:S(2)}, u32[]{:S(2)}) collective-permute-start(bf16[64,2048]{1,0:T(8,128)(2,1)S(1)} %add_convert_fusion), channel_id=1, source_target_pairs={{0,6},{1,7},{2,4},{3,5},{4,2},{5,3},{6,0},{7,1},{8,14},{9,15},{10,... | collective-permute-start | bytes 786440 | tf_op jit(solution)/shard_map/ppermute | solution.py:285
  103.7 0.9 collective-permute-start.19
  104.7 1.4 %collective-permute-start.27 = (bf16[64,2048]{1,0:T(8,128)(2,1)S(1)}, bf16[64,2048]{1,0:T(8,128)(2,1)S(1)}, u32[]{:S(2)}, u32[]{:S(2)}) collective-permute-start(bf16[64,2048]{1,0:T(8,128)(2,1)S(1)} %slice.182), channel_id=1, source_target_pairs={{0,16},{8,24},{16,0},{24,8},{1,17},{9,25},{17,1},{25,9},{2,18},{10... | collective-permute-start | bytes 786440 | tf_op jit(solution)/shard_map/ppermute | solution.py:285
  106.2 5.5 %collective-permute-done.40.refs_3_ = bf16[64,2048]{1,0:T(8,128)(2,1)S(1)} collective-permute-done((bf16[64,2048]{1,0:T(8,128)(2,1)S(1)}, bf16[64,2048]{1,0:T(8,128)(2,1)S(1)}, u32[]{:S(2)}, u32[]{:S(2)}) %collective-permute-start.40) | collective-permute-done | bytes 262176 | tf_op jit(solution)/shard_map/ppermute | solution.py:285
  111.7 1.1 collective-permute-start.9
  112.8 2.2 %collective-permute-done.19.refs_1_ = bf16[64,2048]{1,0:T(8,128)(2,1)S(1)} collective-permute-done((bf16[64,2048]{1,0:T(8,128)(2,1)S(1)}, bf16[64,2048]{1,0:T(8,128)(2,1)S(1)}, u32[]{:S(2)}, u32[]{:S(2)}) %collective-permute-start.19) | collective-permute-done | bytes 262176 | tf_op jit(solution)/shard_map/ppermute | solution.py:285
  115.0 1.4 collective-permute-start.29
  116.5 3.9 %collective-permute-done.29 = bf16[32,2048]{1,0:T(8,128)(2,1)S(1)} collective-permute-done((bf16[32,2048]{1,0:T(8,128)(2,1)S(1)}, bf16[32,2048]{1,0:T(8,128)(2,1)S(1)}, u32[]{:S(2)}, u32[]{:S(2)}) %collective-permute-start.29) | collective-permute-done | bytes 131104 | tf_op jit(solution)/shard_map/ppermute | solution.py:285
  120.6 4.3 %collective-permute-start.30 = (bf16[64,2048]{1,0:T(8,128)(2,1)S(1)}, bf16[64,2048]{1,0:T(8,128)(2,1)S(1)}, u32[]{:S(2)}, u32[]{:S(2)}) collective-permute-start(bf16[64,2048]{1,0:T(8,128)(2,1)S(1)} %add_convert_fusion.1), channel_id=1, source_target_pairs={{0,4},{1,5},{2,6},{3,7},{4,0},{5,1},{6,2},{7,3},{8,12},{9,13},{10,... | collective-permute-start | bytes 786440 | tf_op jit(solution)/shard_map/ppermute | solution.py:285
  124.8 2.3 %grad_out.3 = bf16[1024,1024]{1,0:T(8,128)(2,1)} custom-call(bf16[1024,1024]{1,0:T(8,128)(2,1)} %grad_out.2.refs_0_, bf16[64,2048]{1,0:T(8,128)(2,1)S(1)} %pad_maximum_fusion.refs_0_.refs_1_, bf16[64,2048]{1,0:T(8,128)(2,1)S(1)} %collective-permute-done.1.refs_1_.refs_2_, ...), custom_call_target="tpu_custom_call", output_to_operand_aliasing={{}: (0, {})} | custom-call | flops 1073741824 | bytes 1048576 | tf_op jit(solution)/shard_map/grad_out/pallas_call | solution.py:387
  127.2 0.1 add_convert_fusion.3.refs_0_
  127.3 9.0 %collective-permute-done.30.refs_2_ = bf16[64,2048]{1,0:T(8,128)(2,1)S(1)} collective-permute-done((bf16[64,2048]{1,0:T(8,128)(2,1)S(1)}, bf16[64,2048]{1,0:T(8,128)(2,1)S(1)}, u32[]{:S(2)}, u32[]{:S(2)}) %collective-permute-start.30) | collective-permute-done | bytes 262176 | tf_op jit(solution)/shard_map/ppermute | solution.py:285
  136.3 1.5 %last.1 = (bf16[128,1024]{1,0:T(8,128)(2,1)}, bf16[128,1024]{1,0:T(8,128)(2,1)}) custom-call(s32[128,2]{1,0:T(8,128)S(1)} %get-tuple-element.36.slot_ref, bf16[128,1024]{1,0:T(8,128)(2,1)S(1)} %copy-done, f32[1,1024]{1,0:T(1,128)S(1)} %bitcast.9, f32[128,2]{1,0:T(8,128)S(1)} %get-tuple-element.37.gate_ref, bf16[128,1024]{1,0:T(8,128)(2,1)S(1)} %copy-done.1, ...), custom_call_target="tpu_custom_call" | custom-call | tf_op jit(solution)/shard_map/last/pallas_call | solution.py:408
  (84 shorter events, 1.3 us)
Async XLA Ops:
  2.6 2.1 %collective-permute-start = (bf16[128,2048]{1,0:T(8,128)(2,1)S(1)}, bf16[128,2048]{1,0:T(8,128)(2,1)S(1)}, u32[]{:S(2)}, u32[]{:S(2)}) collective-permute-start(bf16[128,2048]{1,0:T(8,128)(2,1)S(1)} %get-tuple-element.39), channel_id=1, source_target_pairs={{0,1},{1,0},{2,3},{3,2},{4,5},{5,4},{6,7},{7,6},{8,9},{9,8},{10,11... | collective-permute-start | bytes 1572872 | tf_op jit(solution)/shard_map/ppermute | solution.py:285
  3.1 33.2 %copy-start.4 = (bf16[1,1024,1024]{2,1,0:T(8,128)(2,1)S(1)}, bf16[1,1024,1024]{2,1,0:T(8,128)(2,1)}, u32[]{:S(2)}) copy-start(bf16[1,1024,1024]{2,1,0:T(8,128)(2,1)} %param.12) | copy-start | bytes 6291460
  3.2 33.1 %copy-start.3 = (bf16[1,1024,1024]{2,1,0:T(8,128)(2,1)S(1)}, bf16[1,1024,1024]{2,1,0:T(8,128)(2,1)}, u32[]{:S(2)}) copy-start(bf16[1,1024,1024]{2,1,0:T(8,128)(2,1)} %param.11) | copy-start | bytes 6291460
  4.7 9.5 %collective-permute-start.2 = (bf16[64,2048]{1,0:T(8,128)(2,1)S(1)}, bf16[64,2048]{1,0:T(8,128)(2,1)S(1)}, u32[]{:S(2)}, u32[]{:S(2)}) collective-permute-start(bf16[64,2048]{1,0:T(8,128)(2,1)S(1)} %pad_maximum_fusion.refs_0_.refs_1_), channel_id=1, source_target_pairs={{0,16},{8,24},{16,0},{24,8},{1,17},{9,25},{17,1},{25,9},{2,18},{10... | collective-permute-start | bytes 786440 | tf_op jit(solution)/shard_map/ppermute | solution.py:285
  7.7 8.4 %collective-permute-start.1 = (bf16[64,2048]{1,0:T(8,128)(2,1)S(1)}, bf16[64,2048]{1,0:T(8,128)(2,1)S(1)}, u32[]{:S(2)}, u32[]{:S(2)}) collective-permute-start(bf16[64,2048]{1,0:T(8,128)(2,1)S(1)} %pad_maximum_fusion.refs_0_.refs_1_), channel_id=1, source_target_pairs={{0,8},{8,0},{16,24},{24,16},{1,9},{9,1},{17,25},{25,17},{2,10},{10... | collective-permute-start | bytes 786440 | tf_op jit(solution)/shard_map/ppermute | solution.py:285
  9.2 12.6 %collective-permute-start.10 = (bf16[64,2048]{1,0:T(8,128)(2,1)S(1)}, bf16[64,2048]{1,0:T(8,128)(2,1)S(1)}, u32[]{:S(2)}, u32[]{:S(2)}) collective-permute-start(bf16[64,2048]{1,0:T(8,128)(2,1)S(1)} %pad_maximum_fusion.1), channel_id=1, source_target_pairs={{0,2},{1,3},{2,0},{3,1},{4,6},{5,7},{6,4},{7,5},{8,10},{9,11},{10,... | collective-permute-start | bytes 786440 | tf_op jit(solution)/shard_map/ppermute | solution.py:285
  10.9 21.4 %collective-permute-start.20 = (bf16[64,2048]{1,0:T(8,128)(2,1)S(1)}, bf16[64,2048]{1,0:T(8,128)(2,1)S(1)}, u32[]{:S(2)}, u32[]{:S(2)}) collective-permute-start(bf16[64,2048]{1,0:T(8,128)(2,1)S(1)} %pad_maximum_fusion.2), channel_id=1, source_target_pairs={{0,4},{1,5},{2,6},{3,7},{4,0},{5,1},{6,2},{7,3},{8,12},{9,13},{10,... | collective-permute-start | bytes 786440 | tf_op jit(solution)/shard_map/ppermute | solution.py:285
  13.5 19.2 %collective-permute-start.31 = (bf16[64,2048]{1,0:T(8,128)(2,1)S(1)}, bf16[64,2048]{1,0:T(8,128)(2,1)S(1)}, u32[]{:S(2)}, u32[]{:S(2)}) collective-permute-start(bf16[64,2048]{1,0:T(8,128)(2,1)S(1)} %pad_maximum_fusion.3), channel_id=1, source_target_pairs={{0,6},{1,7},{2,4},{3,5},{4,2},{5,3},{6,0},{7,1},{8,14},{9,15},{10,... | collective-permute-start | bytes 786440 | tf_op jit(solution)/shard_map/ppermute | solution.py:285
  14.3 19.0 %collective-permute-start.3 = (bf16[32,2048]{1,0:T(8,128)(2,1)S(1)}, bf16[32,2048]{1,0:T(8,128)(2,1)S(1)}, u32[]{:S(2)}, u32[]{:S(2)}) collective-permute-start(bf16[32,2048]{1,0:T(8,128)(2,1)S(1)} %slice.161), channel_id=1, source_target_pairs={{0,8},{8,0},{16,24},{24,16},{1,9},{9,1},{17,25},{25,17},{2,10},{10... | collective-permute-start | bytes 393224 | tf_op jit(solution)/shard_map/ppermute | solution.py:285
  16.1 18.7 %collective-permute-start.4 = (bf16[32,2048]{1,0:T(8,128)(2,1)S(1)}, bf16[32,2048]{1,0:T(8,128)(2,1)S(1)}, u32[]{:S(2)}, u32[]{:S(2)}) collective-permute-start(bf16[32,2048]{1,0:T(8,128)(2,1)S(1)} %slice.162), channel_id=1, source_target_pairs={{0,16},{8,24},{16,0},{24,8},{1,17},{9,25},{17,1},{25,9},{2,18},{10... | collective-permute-start | bytes 393224 | tf_op jit(solution)/shard_map/ppermute | solution.py:285
  21.7 17.2 %collective-permute-start.12 = (bf16[64,2048]{1,0:T(8,128)(2,1)S(1)}, bf16[64,2048]{1,0:T(8,128)(2,1)S(1)}, u32[]{:S(2)}, u32[]{:S(2)}) collective-permute-start(bf16[64,2048]{1,0:T(8,128)(2,1)S(1)} %collective-permute-done.10.refs_0_.refs_5_.refs_6_), channel_id=1, source_target_pairs={{0,16},{8,24},{16,0},{24,8},{1,17},{9,25},{17,1},{25,9},{2,18},{10... | collective-permute-start | bytes 786440 | tf_op jit(solution)/shard_map/ppermute | solution.py:285
  32.2 8.9 %collective-permute-start.11 = (bf16[64,2048]{1,0:T(8,128)(2,1)S(1)}, bf16[64,2048]{1,0:T(8,128)(2,1)S(1)}, u32[]{:S(2)}, u32[]{:S(2)}) collective-permute-start(bf16[64,2048]{1,0:T(8,128)(2,1)S(1)} %collective-permute-done.10.refs_0_.refs_5_.refs_6_), channel_id=1, source_target_pairs={{0,8},{8,0},{16,24},{24,16},{1,9},{9,1},{17,25},{25,17},{2,10},{10... | collective-permute-start | bytes 786440 | tf_op jit(solution)/shard_map/ppermute | solution.py:285
  32.8 8.4 %collective-permute-start.22 = (bf16[64,2048]{1,0:T(8,128)(2,1)S(1)}, bf16[64,2048]{1,0:T(8,128)(2,1)S(1)}, u32[]{:S(2)}, u32[]{:S(2)}) collective-permute-start(bf16[64,2048]{1,0:T(8,128)(2,1)S(1)} %collective-permute-done.20.refs_0_.refs_10_.refs_11_), channel_id=1, source_target_pairs={{0,16},{8,24},{16,0},{24,8},{1,17},{9,25},{17,1},{25,9},{2,18},{10... | collective-permute-start | bytes 786440 | tf_op jit(solution)/shard_map/ppermute | solution.py:285
  33.3 13.4 %collective-permute-start.21 = (bf16[64,2048]{1,0:T(8,128)(2,1)S(1)}, bf16[64,2048]{1,0:T(8,128)(2,1)S(1)}, u32[]{:S(2)}, u32[]{:S(2)}) collective-permute-start(bf16[64,2048]{1,0:T(8,128)(2,1)S(1)} %collective-permute-done.20.refs_0_.refs_10_.refs_11_), channel_id=1, source_target_pairs={{0,8},{8,0},{16,24},{24,16},{1,9},{9,1},{17,25},{25,17},{2,10},{10... | collective-permute-start | bytes 786440 | tf_op jit(solution)/shard_map/ppermute | solution.py:285
  34.8 11.9 %collective-permute-start.33 = (bf16[64,2048]{1,0:T(8,128)(2,1)S(1)}, bf16[64,2048]{1,0:T(8,128)(2,1)S(1)}, u32[]{:S(2)}, u32[]{:S(2)}) collective-permute-start(bf16[64,2048]{1,0:T(8,128)(2,1)S(1)} %collective-permute-done.31.refs_0_.refs_15_.refs_16_), channel_id=1, source_target_pairs={{0,16},{8,24},{16,0},{24,8},{1,17},{9,25},{17,1},{25,9},{2,18},{10... | collective-permute-start | bytes 786440 | tf_op jit(solution)/shard_map/ppermute | solution.py:285
  39.0 13.4 %collective-permute-start.32 = (bf16[64,2048]{1,0:T(8,128)(2,1)S(1)}, bf16[64,2048]{1,0:T(8,128)(2,1)S(1)}, u32[]{:S(2)}, u32[]{:S(2)}) collective-permute-start(bf16[64,2048]{1,0:T(8,128)(2,1)S(1)} %collective-permute-done.31.refs_0_.refs_15_.refs_16_), channel_id=1, source_target_pairs={{0,8},{8,0},{16,24},{24,16},{1,9},{9,1},{17,25},{25,17},{2,10},{10... | collective-permute-start | bytes 786440 | tf_op jit(solution)/shard_map/ppermute | solution.py:285
  41.1 14.4 %collective-permute-start.6 = (bf16[64,2048]{1,0:T(8,128)(2,1)S(1)}, bf16[64,2048]{1,0:T(8,128)(2,1)S(1)}, u32[]{:S(2)}, u32[]{:S(2)}) collective-permute-start(bf16[64,2048]{1,0:T(8,128)(2,1)S(1)} %get-tuple-element.42), channel_id=1, source_target_pairs={{0,8},{8,0},{16,24},{24,16},{1,9},{9,1},{17,25},{25,17},{2,10},{10... | collective-permute-start | bytes 786440 | tf_op jit(solution)/shard_map/ppermute | solution.py:285
  41.1 39.2 %collective-permute-start.5 = (bf16[128,2048]{1,0:T(8,128)(2,1)S(1)}, bf16[128,2048]{1,0:T(8,128)(2,1)S(1)}, u32[]{:S(2)}, u32[]{:S(2)}) collective-permute-start(bf16[128,2048]{1,0:T(8,128)(2,1)S(1)} %get-tuple-element.41), channel_id=1, source_target_pairs={{0,1},{1,0},{2,3},{3,2},{4,5},{5,4},{6,7},{7,6},{8,9},{9,8},{10,11... | collective-permute-start | bytes 1572872 | tf_op jit(solution)/shard_map/ppermute | solution.py:285
  46.7 16.9 %collective-permute-start.13 = (bf16[32,2048]{1,0:T(8,128)(2,1)S(1)}, bf16[32,2048]{1,0:T(8,128)(2,1)S(1)}, u32[]{:S(2)}, u32[]{:S(2)}) collective-permute-start(bf16[32,2048]{1,0:T(8,128)(2,1)S(1)} %slice.171), channel_id=1, source_target_pairs={{0,8},{8,0},{16,24},{24,16},{1,9},{9,1},{17,25},{25,17},{2,10},{10... | collective-permute-start | bytes 393224 | tf_op jit(solution)/shard_map/ppermute | solution.py:285
  46.7 18.2 %collective-permute-start.14 = (bf16[32,2048]{1,0:T(8,128)(2,1)S(1)}, bf16[32,2048]{1,0:T(8,128)(2,1)S(1)}, u32[]{:S(2)}, u32[]{:S(2)}) collective-permute-start(bf16[32,2048]{1,0:T(8,128)(2,1)S(1)} %slice.172), channel_id=1, source_target_pairs={{0,16},{8,24},{16,0},{24,8},{1,17},{9,25},{17,1},{25,9},{2,18},{10... | collective-permute-start | bytes 393224 | tf_op jit(solution)/shard_map/ppermute | solution.py:285
  52.3 7.3 %collective-permute-start.34 = (bf16[32,2048]{1,0:T(8,128)(2,1)S(1)}, bf16[32,2048]{1,0:T(8,128)(2,1)S(1)}, u32[]{:S(2)}, u32[]{:S(2)}) collective-permute-start(bf16[32,2048]{1,0:T(8,128)(2,1)S(1)} %slice.188), channel_id=1, source_target_pairs={{0,8},{8,0},{16,24},{24,16},{1,9},{9,1},{17,25},{25,17},{2,10},{10... | collective-permute-start | bytes 393224 | tf_op jit(solution)/shard_map/ppermute | solution.py:285
  55.5 5.3 %collective-permute-start.35 = (bf16[32,2048]{1,0:T(8,128)(2,1)S(1)}, bf16[32,2048]{1,0:T(8,128)(2,1)S(1)}, u32[]{:S(2)}, u32[]{:S(2)}) collective-permute-start(bf16[32,2048]{1,0:T(8,128)(2,1)S(1)} %slice.189), channel_id=1, source_target_pairs={{0,16},{8,24},{16,0},{24,8},{1,17},{9,25},{17,1},{25,9},{2,18},{10... | collective-permute-start | bytes 393224 | tf_op jit(solution)/shard_map/ppermute | solution.py:285
  59.7 9.4 %collective-permute-start.23 = (bf16[32,2048]{1,0:T(8,128)(2,1)S(1)}, bf16[32,2048]{1,0:T(8,128)(2,1)S(1)}, u32[]{:S(2)}, u32[]{:S(2)}) collective-permute-start(bf16[32,2048]{1,0:T(8,128)(2,1)S(1)} %slice.178), channel_id=1, source_target_pairs={{0,8},{8,0},{16,24},{24,16},{1,9},{9,1},{17,25},{25,17},{2,10},{10... | collective-permute-start | bytes 393224 | tf_op jit(solution)/shard_map/ppermute | solution.py:285
  60.8 9.5 %collective-permute-start.24 = (bf16[32,2048]{1,0:T(8,128)(2,1)S(1)}, bf16[32,2048]{1,0:T(8,128)(2,1)S(1)}, u32[]{:S(2)}, u32[]{:S(2)}) collective-permute-start(bf16[32,2048]{1,0:T(8,128)(2,1)S(1)} %slice.179), channel_id=1, source_target_pairs={{0,16},{8,24},{16,0},{24,8},{1,17},{9,25},{17,1},{25,9},{2,18},{10... | collective-permute-start | bytes 393224 | tf_op jit(solution)/shard_map/ppermute | solution.py:285
  63.6 18.6 %collective-permute-start.36 = (bf16[64,2048]{1,0:T(8,128)(2,1)S(1)}, bf16[64,2048]{1,0:T(8,128)(2,1)S(1)}, u32[]{:S(2)}, u32[]{:S(2)}) collective-permute-start(bf16[64,2048]{1,0:T(8,128)(2,1)S(1)} %get-tuple-element.54), channel_id=1, source_target_pairs={{0,8},{8,0},{16,24},{24,16},{1,9},{9,1},{17,25},{25,17},{2,10},{10... | collective-permute-start | bytes 786440 | tf_op jit(solution)/shard_map/ppermute | solution.py:285
  64.9 18.3 %collective-permute-start.37 = (bf16[64,2048]{1,0:T(8,128)(2,1)S(1)}, bf16[64,2048]{1,0:T(8,128)(2,1)S(1)}, u32[]{:S(2)}, u32[]{:S(2)}) collective-permute-start(bf16[64,2048]{1,0:T(8,128)(2,1)S(1)} %get-tuple-element.55), channel_id=1, source_target_pairs={{0,16},{8,24},{16,0},{24,8},{1,17},{9,25},{17,1},{25,9},{2,18},{10... | collective-permute-start | bytes 786440 | tf_op jit(solution)/shard_map/ppermute | solution.py:285
  69.1 14.3 %collective-permute-start.15 = (bf16[64,2048]{1,0:T(8,128)(2,1)S(1)}, bf16[64,2048]{1,0:T(8,128)(2,1)S(1)}, u32[]{:S(2)}, u32[]{:S(2)}) collective-permute-start(bf16[64,2048]{1,0:T(8,128)(2,1)S(1)} %get-tuple-element.45), channel_id=1, source_target_pairs={{0,8},{8,0},{16,24},{24,16},{1,9},{9,1},{17,25},{25,17},{2,10},{10... | collective-permute-start | bytes 786440 | tf_op jit(solution)/shard_map/ppermute | solution.py:285
  70.3 13.7 %collective-permute-start.16 = (bf16[64,2048]{1,0:T(8,128)(2,1)S(1)}, bf16[64,2048]{1,0:T(8,128)(2,1)S(1)}, u32[]{:S(2)}, u32[]{:S(2)}) collective-permute-start(bf16[64,2048]{1,0:T(8,128)(2,1)S(1)} %get-tuple-element.46), channel_id=1, source_target_pairs={{0,16},{8,24},{16,0},{24,8},{1,17},{9,25},{17,1},{25,9},{2,18},{10... | collective-permute-start | bytes 786440 | tf_op jit(solution)/shard_map/ppermute | solution.py:285
  80.3 46.9 %collective-permute-start.8 = (bf16[32,2048]{1,0:T(8,128)(2,1)S(1)}, bf16[32,2048]{1,0:T(8,128)(2,1)S(1)}, u32[]{:S(2)}, u32[]{:S(2)}) collective-permute-start(bf16[32,2048]{1,0:T(8,128)(2,1)S(1)} %add_convert_fusion.11), channel_id=1, source_target_pairs={{0,16},{8,24},{16,0},{24,8},{1,17},{9,25},{17,1},{25,9},{2,18},{10... | collective-permute-start | bytes 393224 | tf_op jit(solution)/shard_map/ppermute | solution.py:285
  82.2 6.8 %collective-permute-start.26 = (bf16[64,2048]{1,0:T(8,128)(2,1)S(1)}, bf16[64,2048]{1,0:T(8,128)(2,1)S(1)}, u32[]{:S(2)}, u32[]{:S(2)}) collective-permute-start(bf16[64,2048]{1,0:T(8,128)(2,1)S(1)} %get-tuple-element.51), channel_id=1, source_target_pairs={{0,8},{8,0},{16,24},{24,16},{1,9},{9,1},{17,25},{25,17},{2,10},{10... | collective-permute-start | bytes 786440 | tf_op jit(solution)/shard_map/ppermute | solution.py:285
  83.2 20.5 %collective-permute-start.25 = (bf16[128,2048]{1,0:T(8,128)(2,1)S(1)}, bf16[128,2048]{1,0:T(8,128)(2,1)S(1)}, u32[]{:S(2)}, u32[]{:S(2)}) collective-permute-start(bf16[128,2048]{1,0:T(8,128)(2,1)S(1)} %get-tuple-element.50), channel_id=1, source_target_pairs={{0,1},{1,0},{2,3},{3,2},{4,5},{5,4},{6,7},{7,6},{8,9},{9,8},{10,11... | collective-permute-start | bytes 1572872 | tf_op jit(solution)/shard_map/ppermute | solution.py:285
  83.4 21.3 %collective-permute-start.7 = (bf16[64,2048]{1,0:T(8,128)(2,1)S(1)}, bf16[64,2048]{1,0:T(8,128)(2,1)S(1)}, u32[]{:S(2)}, u32[]{:S(2)}) collective-permute-start(bf16[64,2048]{1,0:T(8,128)(2,1)S(1)} %slice.165), channel_id=1, source_target_pairs={{0,16},{8,24},{16,0},{24,8},{1,17},{9,25},{17,1},{25,9},{2,18},{10... | collective-permute-start | bytes 786440 | tf_op jit(solution)/shard_map/ppermute | solution.py:285
  84.0 10.9 %collective-permute-start.38 = (bf16[32,2048]{1,0:T(8,128)(2,1)S(1)}, bf16[32,2048]{1,0:T(8,128)(2,1)S(1)}, u32[]{:S(2)}, u32[]{:S(2)}) collective-permute-start(bf16[32,2048]{1,0:T(8,128)(2,1)S(1)} %add_convert_fusion.5), channel_id=1, source_target_pairs={{0,16},{8,24},{16,0},{24,8},{1,17},{9,25},{17,1},{25,9},{2,18},{10... | collective-permute-start | bytes 393224 | tf_op jit(solution)/shard_map/ppermute | solution.py:285
  89.0 15.7 %copy-start.5 = (bf16[64,2048]{1,0:T(8,128)(2,1)}, bf16[64,2048]{1,0:T(8,128)(2,1)S(1)}, u32[]{:S(2)}) copy-start(bf16[64,2048]{1,0:T(8,128)(2,1)S(1)} %collective-permute-done.26) | copy-start | bytes 786436
  89.0 6.5 %collective-permute-start.39 = (bf16[32,2048]{1,0:T(8,128)(2,1)S(1)}, bf16[32,2048]{1,0:T(8,128)(2,1)S(1)}, u32[]{:S(2)}, u32[]{:S(2)}) collective-permute-start(bf16[32,2048]{1,0:T(8,128)(2,1)S(1)} %add_convert_fusion.4), channel_id=1, source_target_pairs={{0,8},{8,0},{16,24},{24,16},{1,9},{9,1},{17,25},{25,17},{2,10},{10... | collective-permute-start | bytes 393224 | tf_op jit(solution)/shard_map/ppermute | solution.py:285
  94.9 5.0 %collective-permute-start.17 = (bf16[32,2048]{1,0:T(8,128)(2,1)S(1)}, bf16[32,2048]{1,0:T(8,128)(2,1)S(1)}, u32[]{:S(2)}, u32[]{:S(2)}) collective-permute-start(bf16[32,2048]{1,0:T(8,128)(2,1)S(1)} %add_convert_fusion.9), channel_id=1, source_target_pairs={{0,16},{8,24},{16,0},{24,8},{1,17},{9,25},{17,1},{25,9},{2,18},{10... | collective-permute-start | bytes 393224 | tf_op jit(solution)/shard_map/ppermute | solution.py:285
  95.5 5.1 %collective-permute-start.18 = (bf16[32,2048]{1,0:T(8,128)(2,1)S(1)}, bf16[32,2048]{1,0:T(8,128)(2,1)S(1)}, u32[]{:S(2)}, u32[]{:S(2)}) collective-permute-start(bf16[32,2048]{1,0:T(8,128)(2,1)S(1)} %add_convert_fusion.8), channel_id=1, source_target_pairs={{0,8},{8,0},{16,24},{24,16},{1,9},{9,1},{17,25},{25,17},{2,10},{10... | collective-permute-start | bytes 393224 | tf_op jit(solution)/shard_map/ppermute | solution.py:285
  100.0 16.5 %collective-permute-start.28 = (bf16[32,2048]{1,0:T(8,128)(2,1)S(1)}, bf16[32,2048]{1,0:T(8,128)(2,1)S(1)}, u32[]{:S(2)}, u32[]{:S(2)}) collective-permute-start(bf16[32,2048]{1,0:T(8,128)(2,1)S(1)} %add_convert_fusion.7), channel_id=1, source_target_pairs={{0,16},{8,24},{16,0},{24,8},{1,17},{9,25},{17,1},{25,9},{2,18},{10... | collective-permute-start | bytes 393224 | tf_op jit(solution)/shard_map/ppermute | solution.py:285
  100.7 11.0 %collective-permute-start.40 = (bf16[64,2048]{1,0:T(8,128)(2,1)S(1)}, bf16[64,2048]{1,0:T(8,128)(2,1)S(1)}, u32[]{:S(2)}, u32[]{:S(2)}) collective-permute-start(bf16[64,2048]{1,0:T(8,128)(2,1)S(1)} %add_convert_fusion), channel_id=1, source_target_pairs={{0,6},{1,7},{2,4},{3,5},{4,2},{5,3},{6,0},{7,1},{8,14},{9,15},{10,... | collective-permute-start | bytes 786440 | tf_op jit(solution)/shard_map/ppermute | solution.py:285
  103.7 11.2 %collective-permute-start.19 = (bf16[64,2048]{1,0:T(8,128)(2,1)S(1)}, bf16[64,2048]{1,0:T(8,128)(2,1)S(1)}, u32[]{:S(2)}, u32[]{:S(2)}) collective-permute-start(bf16[64,2048]{1,0:T(8,128)(2,1)S(1)} %add_convert_fusion.2), channel_id=1, source_target_pairs={{0,2},{1,3},{2,0},{3,1},{4,6},{5,7},{6,4},{7,5},{8,10},{9,11},{10,... | collective-permute-start | bytes 786440 | tf_op jit(solution)/shard_map/ppermute | solution.py:285
  104.7 15.7 %slice-start = ((bf16[64,2048]{1,0:T(8,128)(2,1)}), bf16[32,2048]{1,0:T(8,128)(2,1)S(1)}, s32[]{:S(2)}) async-start(bf16[64,2048]{1,0:T(8,128)(2,1)} %copy-done.5), calls=%async_computation | async-start | bytes 262144 | tf_op jit(solution)/shard_map/slice | solution.py:369
  104.7 10.3 %collective-permute-start.27 = (bf16[64,2048]{1,0:T(8,128)(2,1)S(1)}, bf16[64,2048]{1,0:T(8,128)(2,1)S(1)}, u32[]{:S(2)}, u32[]{:S(2)}) collective-permute-start(bf16[64,2048]{1,0:T(8,128)(2,1)S(1)} %slice.182), channel_id=1, source_target_pairs={{0,16},{8,24},{16,0},{24,8},{1,17},{9,25},{17,1},{25,9},{2,18},{10... | collective-permute-start | bytes 786440 | tf_op jit(solution)/shard_map/ppermute | solution.py:285
  111.7 15.5 %collective-permute-start.9 = (bf16[32,2048]{1,0:T(8,128)(2,1)S(1)}, bf16[32,2048]{1,0:T(8,128)(2,1)S(1)}, u32[]{:S(2)}, u32[]{:S(2)}) collective-permute-start(bf16[32,2048]{1,0:T(8,128)(2,1)S(1)} %add_convert_fusion.10), channel_id=1, source_target_pairs={{0,8},{8,0},{16,24},{24,16},{1,9},{9,1},{17,25},{25,17},{2,10},{10... | collective-permute-start | bytes 393224 | tf_op jit(solution)/shard_map/ppermute | solution.py:285
  115.0 5.4 %collective-permute-start.29 = (bf16[32,2048]{1,0:T(8,128)(2,1)S(1)}, bf16[32,2048]{1,0:T(8,128)(2,1)S(1)}, u32[]{:S(2)}, u32[]{:S(2)}) collective-permute-start(bf16[32,2048]{1,0:T(8,128)(2,1)S(1)} %add_convert_fusion.6), channel_id=1, source_target_pairs={{0,8},{8,0},{16,24},{24,16},{1,9},{9,1},{17,25},{25,17},{2,10},{10... | collective-permute-start | bytes 393224 | tf_op jit(solution)/shard_map/ppermute | solution.py:285
  116.4 10.9 %collective-permute-start.41 = (bf16[64,2048]{1,0:T(8,128)(2,1)S(1)}, bf16[64,2048]{1,0:T(8,128)(2,1)S(1)}, u32[]{:S(2)}, u32[]{:S(2)}) collective-permute-start(bf16[64,2048]{1,0:T(8,128)(2,1)S(1)} %pad_maximum_fusion.4), channel_id=1, source_target_pairs={{0,1},{1,0},{2,3},{3,2},{4,5},{5,4},{6,7},{7,6},{8,9},{9,8},{10,11... | collective-permute-start | bytes 786440 | tf_op jit(solution)/shard_map/ppermute | solution.py:285
  120.5 15.8 %copy-start = (bf16[128,1024]{1,0:T(8,128)(2,1)S(1)}, bf16[128,1024]{1,0:T(8,128)(2,1)}, u32[]{:S(2)}) copy-start(bf16[128,1024]{1,0:T(8,128)(2,1)} %tok_ref.1) | copy-start | bytes 786436
  120.5 15.8 %copy-start.1 = (bf16[128,1024]{1,0:T(8,128)(2,1)S(1)}, bf16[128,1024]{1,0:T(8,128)(2,1)}, u32[]{:S(2)}) copy-start(bf16[128,1024]{1,0:T(8,128)(2,1)} %cot_ref.1) | copy-start | bytes 786436
  120.6 15.8 %copy-start.2 = (f32[1024]{0:T(1024)S(1)}, f32[1024]{0:T(1024)}, u32[]{:S(2)}) copy-start(f32[1024]{0:T(1024)} %param.8) | copy-start | bytes 12292
  120.6 15.7 %collective-permute-start.30 = (bf16[64,2048]{1,0:T(8,128)(2,1)S(1)}, bf16[64,2048]{1,0:T(8,128)(2,1)S(1)}, u32[]{:S(2)}, u32[]{:S(2)}) collective-permute-start(bf16[64,2048]{1,0:T(8,128)(2,1)S(1)} %add_convert_fusion.1), channel_id=1, source_target_pairs={{0,4},{1,5},{2,6},{3,7},{4,0},{5,1},{6,2},{7,3},{8,12},{9,13},{10,... | collective-permute-start | bytes 786440 | tf_op jit(solution)/shard_map/ppermute | solution.py:285

commit v2 on v1

--- a/solution.py
+++ b/solution.py
@@ -171,14 +171,15 @@
 
 
 def expert_kernel(pieces, form, *refs):
-    parts, (w1_ref, w2_ref), outs = refs[:pieces], refs[pieces : pieces + 2], refs[pieces + 2 : -2]
-    hid_ref, pre_ref = refs[-2:]
+    parts, (w1_ref, w2_ref), outs = refs[:pieces], refs[pieces : pieces + 2], refs[pieces + 2 : -4]
+    x_ref, d_ref, hid_ref, pre_ref = refs[-4:]
     count, width = parts[0].shape
     features = width // 2
     hidden_units = w1_ref.shape[1]
     tile = min(256, hidden_units)
     x_rows = jnp.concatenate([p[:, :features] for p in parts], axis=0)
     d_rows = jnp.concatenate([p[:, features:] for p in parts], axis=0)
+    x_ref[...], d_ref[...] = x_rows, d_rows
     for j in range(0, hidden_units, tile):
         at = slice(j, j + tile)
         v = dot_nn(x_rows, w1_ref[:, at])
@@ -223,21 +224,16 @@
             outs[out][there, features + j : features + j + tile] = dx[rows]
 
 
-def grad_kernel(pieces, chips, first, base, *refs):
+def grad_kernel(chips, base, *refs):
     if base:
         refs = refs[1:]
-    rows, tall, out_ref = refs[:pieces], refs[pieces : pieces + chips], refs[pieces + chips]
-    step = pl.program_id(0) + base
+    left, right, out_ref = refs[:chips], refs[chips : 2 * chips], refs[2 * chips]
     tile = out_ref.shape[0]
-    features = rows[0].shape[1] // 2
-    at = pl.ds(pl.multiple_of(step * tile, tile), tile)
-    if first:
-        left = jnp.concatenate([r[:, at] for r in rows], axis=0)
-        right = jnp.concatenate([r[...] for r in tall], axis=0)
-    else:
-        left = jnp.concatenate([r[:, at] for r in tall], axis=0)
-        right = jnp.concatenate([r[:, features:] for r in rows], axis=0)
-    out_ref[...] = dot_tn(left, right).astype(BF16)
+    at = pl.ds(pl.multiple_of((pl.program_id(0) + base) * tile, tile), tile)
+    total = dot_tn(left[0][:, at], right[0][...])
+    for k in range(1, chips):
+        total = total + dot_tn(left[k][:, at], right[k][...])
+    out_ref[...] = total.astype(BF16)
 
 
 def last_kernel(capacity, chips, late, slot_ref, tok_ref, gain_ref, gate_ref, cot_ref, *refs):
@@ -342,15 +338,17 @@
             sizes = (capacity, count, capacity, 2 * count)
         else:
             sizes = (count, count, count, capacity, capacity) if SCATTER[k] == 2 else (count, 2 * count, count)
-        *leaving, hid, pre = call(
+        *leaving, x_all, d_all, hid, pre = call(
             functools.partial(expert_kernel, len(rows[k]), SCATTER[k]),
-            tuple(((n, wide), BF16) for n in sizes) + (((4 * count, units), BF16),) * 2,
+            tuple(((n, wide), BF16) for n in sizes)
+            + (((4 * count, features), BF16),) * 2
+            + (((4 * count, units), BF16),) * 2,
             (*rows[k], w_first, w_second),
             cost_estimate=pl.CostEstimate(
                 flops=8 * 4 * count * features * units, bytes_accessed=4 * features * units, transcendentals=0
             ),
         )
-        tall[k], parts[k] = (hid, pre), leaving
+        tall[k], parts[k] = ((hid, d_all), (x_all, pre)), leaving
     back = {}
     for k in range(chips):
         if SCATTER[k] >= 2:
@@ -376,16 +374,15 @@
             summed = (f32(own) + f32(got[:count]) + f32(last)).astype(BF16)
         back[k] = flip(summed, "exp", 2 * k) if k else summed
     grads = []
-    pieces = [r for k in range(chips) for r in rows[k]]
     for first in (False, True):
-        args = [vmem(a) for a in pieces + [tall[k][1 if first else 0] for k in range(chips)]]
+        args = [vmem(tall[k][first][i]) for i in range(2) for k in range(chips)]
         size = (features, units) if first else (units, features)
         tile = min(256, size[0])
         steps = size[0] // tile
         done = None
         for base in (0, steps // 2):
             done = pl.pallas_call(
-                functools.partial(grad_kernel, len(pieces), chips, first, base),
+                functools.partial(grad_kernel, chips, base),
                 out_shape=jax.ShapeDtypeStruct(size, BF16),
                 grid=(steps - base if base else steps // 2,),
                 in_specs=([pl.BlockSpec(memory_space=pl.ANY)] if base else []) + [spec] * len(args),

time: 138 us -> 145 us (1.051)
  waiting for transfers between devices: 67.7 us -> 77.6 us
  starting transfers between devices: 44.4 us -> 41.7 us
    ppermute x42, waiting for transfers between devices: 67.7 us -> 77.6 us  [flip(): return lax.ppermute(array, axis_name, [(i, i ^ mask) for i in range(size)])]
    ppermute x42, starting transfers between devices: 44.4 us -> 41.7 us  [flip(): return lax.ppermute(array, axis_name, [(i, i ^ mask) for i in range(size)])]
  transfers between devices with their start and end apart: 42 -> 42, of which waited for: 17 -> 19; matrix products, arithmetic and copies ran while one was open for 1% -> 1% of each run, Pallas kernels for 15% -> 14%
where the time goes in v2:
time: 145 us
  waiting for transfers between devices  77.6 us (54%)
  starting transfers between devices  41.7 us (29%)
  Pallas kernels  23.5 us (16%)
    ppermute x42, waiting for transfers between devices, flip(): return lax.ppermute(array, axis_name, [(i, i ^ mask) for i in range(size)])  77.6 us
    ppermute x42, starting transfers between devices, flip(): return lax.ppermute(array, axis_name, [(i, i ^ mask) for i in range(size)])  41.7 us
    pallas_call x4, Pallas kernels, call(): pl.pallas_call(kernel, out_shape=tuple((pltpu.VMEM(s, d) for s, d in outs...  10.8 us
    pallas_call x4, Pallas kernels, local_inner(): pl.pallas_call(functools.partial(grad_kernel, chips, base), out_shape=jax...  9.25 us
  transfers between devices with their start and end apart: 42, of which 19 were waited for; matrix products, arithmetic and copies ran while one was open for 1% of the time, Pallas kernels for 14%

profile of v2, /device:TPU:0, one launch (start us, length us, event | category | flops | bytes accessed | tf_op | source)
XLA Modules:
  0.0 144.9 jit_solution(8582105994089728418)
XLA Ops:
  0.6 1.9 %send.1 = (bf16[128,2048]{1,0:T(8,128)(2,1)S(1)}, bf16[128,2048]{1,0:T(8,128)(2,1)S(1)}, s32[128,2]{1,0:T(8,128)S(1)}, f32[128,2]{1,0:T(8,128)S(1)}) custom-call(s32[1]{0:T(128)} %bitcast.me_ref, s32[2,128]{1,0:T(2,128)} %bitcast.20, f32[2,128]{1,0:T(2,128)} %bitcast.21, bf16[128,1024]{1,0:T(8,128)(2,1)} %tok_ref.1, f32[1,1024]{1,0:T(1,128)} %bitcast.8, ...), custom_call_target="tpu_custom_call" | custom-call | tf_op jit(solution)/shard_map/send/pallas_call | solution.py:304
  2.6 0.6 collective-permute-start
  3.2 1.5 %collective-permute-done = bf16[128,2048]{1,0:T(8,128)(2,1)S(1)} collective-permute-done((bf16[128,2048]{1,0:T(8,128)(2,1)S(1)}, bf16[128,2048]{1,0:T(8,128)(2,1)S(1)}, u32[]{:S(2)}, u32[]{:S(2)}) %collective-permute-start) | collective-permute-done | bytes 524320 | tf_op jit(solution)/shard_map/ppermute | solution.py:281
  4.7 2.9 %collective-permute-start.2 = (bf16[64,2048]{1,0:T(8,128)(2,1)S(1)}, bf16[64,2048]{1,0:T(8,128)(2,1)S(1)}, u32[]{:S(2)}, u32[]{:S(2)}) collective-permute-start(bf16[64,2048]{1,0:T(8,128)(2,1)S(1)} %pad_maximum_fusion.refs_0_), channel_id=1, source_target_pairs={{0,16},{8,24},{16,0},{24,8},{1,17},{9,25},{17,1},{25,9},{2,18},{10... | collective-permute-start | bytes 786440 | tf_op jit(solution)/shard_map/ppermute | solution.py:281
  7.7 1.5 %collective-permute-start.1 = (bf16[64,2048]{1,0:T(8,128)(2,1)S(1)}, bf16[64,2048]{1,0:T(8,128)(2,1)S(1)}, u32[]{:S(2)}, u32[]{:S(2)}) collective-permute-start(bf16[64,2048]{1,0:T(8,128)(2,1)S(1)} %pad_maximum_fusion.refs_0_), channel_id=1, source_target_pairs={{0,8},{8,0},{16,24},{24,16},{1,9},{9,1},{17,25},{25,17},{2,10},{10... | collective-permute-start | bytes 786440 | tf_op jit(solution)/shard_map/ppermute | solution.py:281
  9.2 1.6 %collective-permute-start.10 = (bf16[64,2048]{1,0:T(8,128)(2,1)S(1)}, bf16[64,2048]{1,0:T(8,128)(2,1)S(1)}, u32[]{:S(2)}, u32[]{:S(2)}) collective-permute-start(bf16[64,2048]{1,0:T(8,128)(2,1)S(1)} %pad_maximum_fusion.1), channel_id=1, source_target_pairs={{0,2},{1,3},{2,0},{3,1},{4,6},{5,7},{6,4},{7,5},{8,10},{9,11},{10,... | collective-permute-start | bytes 786440 | tf_op jit(solution)/shard_map/ppermute | solution.py:281
  10.9 2.7 %collective-permute-start.20 = (bf16[64,2048]{1,0:T(8,128)(2,1)S(1)}, bf16[64,2048]{1,0:T(8,128)(2,1)S(1)}, u32[]{:S(2)}, u32[]{:S(2)}) collective-permute-start(bf16[64,2048]{1,0:T(8,128)(2,1)S(1)} %pad_maximum_fusion.2), channel_id=1, source_target_pairs={{0,4},{1,5},{2,6},{3,7},{4,0},{5,1},{6,2},{7,3},{8,12},{9,13},{10,... | collective-permute-start | bytes 786440 | tf_op jit(solution)/shard_map/ppermute | solution.py:281
  13.5 0.3 collective-permute-start.31
  13.8 0.5 collective-permute-done.2.refs_2_
  14.3 1.8 %collective-permute-start.3 = (bf16[32,2048]{1,0:T(8,128)(2,1)S(1)}, bf16[32,2048]{1,0:T(8,128)(2,1)S(1)}, u32[]{:S(2)}, u32[]{:S(2)}) collective-permute-start(bf16[32,2048]{1,0:T(8,128)(2,1)S(1)} %slice.161), channel_id=1, source_target_pairs={{0,8},{8,0},{16,24},{24,16},{1,9},{9,1},{17,25},{25,17},{2,10},{10... | collective-permute-start | bytes 393224 | tf_op jit(solution)/shard_map/ppermute | solution.py:281
  16.1 1.6 %collective-permute-start.4 = (bf16[32,2048]{1,0:T(8,128)(2,1)S(1)}, bf16[32,2048]{1,0:T(8,128)(2,1)S(1)}, u32[]{:S(2)}, u32[]{:S(2)}) collective-permute-start(bf16[32,2048]{1,0:T(8,128)(2,1)S(1)} %slice.162), channel_id=1, source_target_pairs={{0,16},{8,24},{16,0},{24,8},{1,17},{9,25},{17,1},{25,9},{2,18},{10... | collective-permute-start | bytes 393224 | tf_op jit(solution)/shard_map/ppermute | solution.py:281
  17.7 4.1 %collective-permute-done.10.refs_0_ = bf16[64,2048]{1,0:T(8,128)(2,1)S(1)} collective-permute-done((bf16[64,2048]{1,0:T(8,128)(2,1)S(1)}, bf16[64,2048]{1,0:T(8,128)(2,1)S(1)}, u32[]{:S(2)}, u32[]{:S(2)}) %collective-permute-start.10) | collective-permute-done | bytes 262176 | tf_op jit(solution)/shard_map/ppermute | solution.py:281
  21.7 0.5 collective-permute-start.12
  22.3 10.0 %collective-permute-done.20.refs_0_ = bf16[64,2048]{1,0:T(8,128)(2,1)S(1)} collective-permute-done((bf16[64,2048]{1,0:T(8,128)(2,1)S(1)}, bf16[64,2048]{1,0:T(8,128)(2,1)S(1)}, u32[]{:S(2)}, u32[]{:S(2)}) %collective-permute-start.20) | collective-permute-done | bytes 262176 | tf_op jit(solution)/shard_map/ppermute | solution.py:281
  32.2 0.5 collective-permute-start.11
  32.8 0.5 collective-permute-start.22
  33.3 1.5 %collective-permute-start.21 = (bf16[64,2048]{1,0:T(8,128)(2,1)S(1)}, bf16[64,2048]{1,0:T(8,128)(2,1)S(1)}, u32[]{:S(2)}, u32[]{:S(2)}) collective-permute-start(bf16[64,2048]{1,0:T(8,128)(2,1)S(1)} %collective-permute-done.20.refs_0_), channel_id=1, source_target_pairs={{0,8},{8,0},{16,24},{24,16},{1,9},{9,1},{17,25},{25,17},{2,10},{10... | collective-permute-start | bytes 786440 | tf_op jit(solution)/shard_map/ppermute | solution.py:281
  34.8 1.5 %collective-permute-start.33 = (bf16[64,2048]{1,0:T(8,128)(2,1)S(1)}, bf16[64,2048]{1,0:T(8,128)(2,1)S(1)}, u32[]{:S(2)}, u32[]{:S(2)}) collective-permute-start(bf16[64,2048]{1,0:T(8,128)(2,1)S(1)} %collective-permute-done.31.refs_0_), channel_id=1, source_target_pairs={{0,16},{8,24},{16,0},{24,8},{1,17},{9,25},{17,1},{25,9},{2,18},{10... | collective-permute-start | bytes 786440 | tf_op jit(solution)/shard_map/ppermute | solution.py:281
  36.3 2.7 %shard_map.102 = (bf16[32,2048]{1,0:T(8,128)(2,1)S(1)}, bf16[64,2048]{1,0:T(8,128)(2,1)S(1)}, bf16[32,2048]{1,0:T(8,128)(2,1)S(1)}, bf16[128,2048]{1,0:T(8,128)(...) custom-call(bf16[64,2048]{1,0:T(8,128)(2,1)S(1)} %pad_maximum_fusion, ...), custom_call_target="tpu_custom_call" | custom-call | flops 2147483648 | bytes 4194304 | tf_op jit(solution)/shard_map/pallas_call | solution.py:269
  39.0 0.6 collective-permute-start.32
  39.6 1.5 %collective-permute-done.11.refs_1_ = bf16[64,2048]{1,0:T(8,128)(2,1)S(1)} collective-permute-done((bf16[64,2048]{1,0:T(8,128)(2,1)S(1)}, bf16[64,2048]{1,0:T(8,128)(2,1)S(1)}, u32[]{:S(2)}, u32[]{:S(2)}) %collective-permute-start.11) | collective-permute-done | bytes 262176 | tf_op jit(solution)/shard_map/ppermute | solution.py:281
  41.2 5.5 %collective-permute-done.21.refs_1_ = bf16[64,2048]{1,0:T(8,128)(2,1)S(1)} collective-permute-done((bf16[64,2048]{1,0:T(8,128)(2,1)S(1)}, bf16[64,2048]{1,0:T(8,128)(2,1)S(1)}, u32[]{:S(2)}, u32[]{:S(2)}) %collective-permute-start.21) | collective-permute-done | bytes 262176 | tf_op jit(solution)/shard_map/ppermute | solution.py:281
  46.7 0.6 collective-permute-start.14
  47.3 5.0 %collective-permute-done.32.refs_1_ = bf16[64,2048]{1,0:T(8,128)(2,1)S(1)} collective-permute-done((bf16[64,2048]{1,0:T(8,128)(2,1)S(1)}, bf16[64,2048]{1,0:T(8,128)(2,1)S(1)}, u32[]{:S(2)}, u32[]{:S(2)}) %collective-permute-start.32) | collective-permute-done | bytes 262176 | tf_op jit(solution)/shard_map/ppermute | solution.py:281
  52.3 3.1 %collective-permute-done.6 = bf16[64,2048]{1,0:T(8,128)(2,1)S(1)} collective-permute-done((bf16[64,2048]{1,0:T(8,128)(2,1)S(1)}, bf16[64,2048]{1,0:T(8,128)(2,1)S(1)}, u32[]{:S(2)}, u32[]{:S(2)}) %collective-permute-start.6) | collective-permute-done | bytes 262176 | tf_op jit(solution)/shard_map/ppermute | solution.py:281
  55.5 0.5 collective-permute-start.24
  56.0 3.7 %collective-permute-done.23.refs_3_ = bf16[32,2048]{1,0:T(8,128)(2,1)S(1)} collective-permute-done((bf16[32,2048]{1,0:T(8,128)(2,1)S(1)}, bf16[32,2048]{1,0:T(8,128)(2,1)S(1)}, u32[]{:S(2)}, u32[]{:S(2)}) %collective-permute-start.23) | collective-permute-done | bytes 131104 | tf_op jit(solution)/shard_map/ppermute | solution.py:281
  59.7 0.5 collective-permute-start.34
  60.4 0.5 collective-permute-start.35
  60.9 2.7 %shard_map.104 = (bf16[32,2048]{1,0:T(8,128)(2,1)S(1)}, bf16[64,2048]{1,0:T(8,128)(2,1)S(1)}, bf16[32,2048]{1,0:T(8,128)(2,1)S(1)}, bf16[128,2048]{1,0:T(8,128)(...) custom-call(bf16[64,2048]{1,0:T(8,128)(2,1)S(1)} %collective-permute, ...), custom_call_target="tpu_custom_call" | custom-call | flops 2147483648 | bytes 4194304 | tf_op jit(solution)/shard_map/pallas_call | solution.py:269
  63.6 2.0 %collective-permute-done.34.refs_3_ = bf16[32,2048]{1,0:T(8,128)(2,1)S(1)} collective-permute-done((bf16[32,2048]{1,0:T(8,128)(2,1)S(1)}, bf16[32,2048]{1,0:T(8,128)(2,1)S(1)}, u32[]{:S(2)}, u32[]{:S(2)}) %collective-permute-start.34) | collective-permute-done | bytes 131104 | tf_op jit(solution)/shard_map/ppermute | solution.py:281
  65.7 0.9 collective-permute-start.8
  66.6 0.4 collective-permute-start.26
  66.9 2.7 %shard_map.105 = (bf16[64,2048]{1,0:T(8,128)(2,1)S(1)}, bf16[64,2048]{1,0:T(8,128)(2,1)S(1)}, bf16[64,2048]{1,0:T(8,128)(2,1)S(1)}, bf16[32,2048]{1,0:T(8,128)(2...) custom-call(bf16[64,2048]{1,0:T(8,128)(2,1)S(1)} %collective-permute, ...), custom_call_target="tpu_custom_call" | custom-call | flops 2147483648 | bytes 4194304 | tf_op jit(solution)/shard_map/pallas_call | solution.py:269
  69.7 1.7 %collective-permute-start.36 = (bf16[64,2048]{1,0:T(8,128)(2,1)S(1)}, bf16[64,2048]{1,0:T(8,128)(2,1)S(1)}, u32[]{:S(2)}, u32[]{:S(2)}) collective-permute-start(bf16[64,2048]{1,0:T(8,128)(2,1)S(1)} %get-tuple-element.62), channel_id=1, source_target_pairs={{0,8},{8,0},{16,24},{24,16},{1,9},{9,1},{17,25},{25,17},{2,10},{10... | collective-permute-start | bytes 786440 | tf_op jit(solution)/shard_map/ppermute | solution.py:281
  71.4 2.8 %shard_map.103 = (bf16[64,2048]{1,0:T(8,128)(2,1)S(1)}, bf16[64,2048]{1,0:T(8,128)(2,1)S(1)}, bf16[64,2048]{1,0:T(8,128)(2,1)S(1)}, bf16[32,2048]{1,0:T(8,128)(2...) custom-call(bf16[64,2048]{1,0:T(8,128)(2,1)S(1)} %collective-permute, ...), custom_call_target="tpu_custom_call" | custom-call | flops 2147483648 | bytes 4194304 | tf_op jit(solution)/shard_map/pallas_call | solution.py:269
  74.3 2.3 %grad_in.2.refs_0_ = bf16[1024,1024]{1,0:T(8,128)(2,1)} custom-call(bf16[256,1024]{1,0:T(8,128)(2,1)S(1)} %get-tuple-element.68.refs_0_.refs_1_, bf16[256,1024]{1,0:T(8,128)(2,1)S(1)} %get-tuple-element.69.refs_1_.refs_2_, bf16[256,1024]{1,0:T(8,128)(2,1)S(1)} %get-tuple-element.70.refs_2_.refs_3_, bf16[256,1024]{1,0:T(8,128)(2,1)S(1)} %get-tuple-element.71.refs_3_.refs_4_, ...), custom_call_target="tpu_custom_call" | custom-call | flops 1073741824 | bytes 1048576 | tf_op jit(solution)/shard_map/grad_in/pallas_call | solution.py:384
  76.6 2.3 %grad_in.3 = bf16[1024,1024]{1,0:T(8,128)(2,1)} custom-call(bf16[1024,1024]{1,0:T(8,128)(2,1)} %grad_in.2.refs_0_, bf16[256,1024]{1,0:T(8,128)(2,1)S(1)} %get-tuple-element.68.refs_0_.refs_1_, bf16[256,1024]{1,0:T(8,128)(2,1)S(1)} %get-tuple-element.69.refs_1_.refs_2_, ...), custom_call_target="tpu_custom_call", output_to_operand_aliasing={{}: (0, {})} | custom-call | flops 1073741824 | bytes 1048576 | tf_op jit(solution)/shard_map/grad_in/pallas_call | solution.py:384
  78.9 2.3 %grad_out.2.refs_0_ = bf16[1024,1024]{1,0:T(8,128)(2,1)} custom-call(bf16[256,1024]{1,0:T(8,128)(2,1)S(1)} %get-tuple-element.76.refs_0_.refs_1_, bf16[256,1024]{1,0:T(8,128)(2,1)S(1)} %get-tuple-element.77.refs_1_.refs_2_, bf16[256,1024]{1,0:T(8,128)(2,1)S(1)} %get-tuple-element.78.refs_2_.refs_3_, bf16[256,1024]{1,0:T(8,128)(2,1)S(1)} %get-tuple-element.79.refs_3_.refs_4_, ...), custom_call_target="tpu_custom_call" | custom-call | flops 1073741824 | bytes 1048576 | tf_op jit(solution)/shard_map/grad_out/pallas_call | solution.py:384
  81.2 1.1 collective-permute-start.37
  82.4 1.0 collective-permute-start.15
  83.4 0.4 collective-permute-start.16
  83.9 6.5 %collective-permute-done.37 = bf16[64,2048]{1,0:T(8,128)(2,1)S(1)} collective-permute-done((bf16[64,2048]{1,0:T(8,128)(2,1)S(1)}, bf16[64,2048]{1,0:T(8,128)(2,1)S(1)}, u32[]{:S(2)}, u32[]{:S(2)}) %collective-permute-start.37) | collective-permute-done | bytes 262176 | tf_op jit(solution)/shard_map/ppermute | solution.py:281
  90.4 1.1 collective-permute-start.7
  91.6 1.0 collective-permute-start.38
  92.6 3.4 %collective-permute-done.16 = bf16[64,2048]{1,0:T(8,128)(2,1)S(1)} collective-permute-done((bf16[64,2048]{1,0:T(8,128)(2,1)S(1)}, bf16[64,2048]{1,0:T(8,128)(2,1)S(1)}, u32[]{:S(2)}, u32[]{:S(2)}) %collective-permute-start.16) | collective-permute-done | bytes 262176 | tf_op jit(solution)/shard_map/ppermute | solution.py:281
  96.0 0.4 collective-permute-start.39
  96.5 7.1 %collective-permute-done.38 = bf16[32,2048]{1,0:T(8,128)(2,1)S(1)} collective-permute-done((bf16[32,2048]{1,0:T(8,128)(2,1)S(1)}, bf16[32,2048]{1,0:T(8,128)(2,1)S(1)}, u32[]{:S(2)}, u32[]{:S(2)}) %collective-permute-start.38) | collective-permute-done | bytes 131104 | tf_op jit(solution)/shard_map/ppermute | solution.py:281
  103.6 1.1 collective-permute-start.17
  104.7 0.9 collective-permute-start.18
  105.8 2.8 %collective-permute-done.17 = bf16[32,2048]{1,0:T(8,128)(2,1)S(1)} collective-permute-done((bf16[32,2048]{1,0:T(8,128)(2,1)S(1)}, bf16[32,2048]{1,0:T(8,128)(2,1)S(1)}, u32[]{:S(2)}, u32[]{:S(2)}) %collective-permute-start.17) | collective-permute-done | bytes 131104 | tf_op jit(solution)/shard_map/ppermute | solution.py:281
  108.6 1.1 collective-permute-start.28
  109.7 1.1 collective-permute-start.40
  110.9 2.3 %collective-permute-start.19 = (bf16[64,2048]{1,0:T(8,128)(2,1)S(1)}, bf16[64,2048]{1,0:T(8,128)(2,1)S(1)}, u32[]{:S(2)}, u32[]{:S(2)}) collective-permute-start(bf16[64,2048]{1,0:T(8,128)(2,1)S(1)} %add_convert_fusion.2), channel_id=1, source_target_pairs={{0,2},{1,3},{2,0},{3,1},{4,6},{5,7},{6,4},{7,5},{8,10},{9,11},{10,... | collective-permute-start | bytes 786440 | tf_op jit(solution)/shard_map/ppermute | solution.py:281
  113.3 1.0 collective-permute-start.27
  114.4 6.3 %collective-permute-done.40.refs_3_ = bf16[64,2048]{1,0:T(8,128)(2,1)S(1)} collective-permute-done((bf16[64,2048]{1,0:T(8,128)(2,1)S(1)}, bf16[64,2048]{1,0:T(8,128)(2,1)S(1)}, u32[]{:S(2)}, u32[]{:S(2)}) %collective-permute-start.40) | collective-permute-done | bytes 262176 | tf_op jit(solution)/shard_map/ppermute | solution.py:281
  120.7 0.9 collective-permute-start.9
  121.6 1.6 %collective-permute-done.19.refs_1_ = bf16[64,2048]{1,0:T(8,128)(2,1)S(1)} collective-permute-done((bf16[64,2048]{1,0:T(8,128)(2,1)S(1)}, bf16[64,2048]{1,0:T(8,128)(2,1)S(1)}, u32[]{:S(2)}, u32[]{:S(2)}) %collective-permute-start.19) | collective-permute-done | bytes 262176 | tf_op jit(solution)/shard_map/ppermute | solution.py:281
  123.3 1.3 collective-permute-start.29
  124.7 3.8 %collective-permute-done.29 = bf16[32,2048]{1,0:T(8,128)(2,1)S(1)} collective-permute-done((bf16[32,2048]{1,0:T(8,128)(2,1)S(1)}, bf16[32,2048]{1,0:T(8,128)(2,1)S(1)}, u32[]{:S(2)}, u32[]{:S(2)}) %collective-permute-start.29) | collective-permute-done | bytes 131104 | tf_op jit(solution)/shard_map/ppermute | solution.py:281
  128.6 3.4 %collective-permute-start.30 = (bf16[64,2048]{1,0:T(8,128)(2,1)S(1)}, bf16[64,2048]{1,0:T(8,128)(2,1)S(1)}, u32[]{:S(2)}, u32[]{:S(2)}) collective-permute-start(bf16[64,2048]{1,0:T(8,128)(2,1)S(1)} %add_convert_fusion.1), channel_id=1, source_target_pairs={{0,4},{1,5},{2,6},{3,7},{4,0},{5,1},{6,2},{7,3},{8,12},{9,13},{10,... | collective-permute-start | bytes 786440 | tf_op jit(solution)/shard_map/ppermute | solution.py:281
  132.0 2.3 %grad_out.3 = bf16[1024,1024]{1,0:T(8,128)(2,1)} custom-call(bf16[1024,1024]{1,0:T(8,128)(2,1)} %grad_out.2.refs_0_, bf16[256,1024]{1,0:T(8,128)(2,1)S(1)} %get-tuple-element.76.refs_0_.refs_1_, bf16[256,1024]{1,0:T(8,128)(2,1)S(1)} %get-tuple-element.77.refs_1_.refs_2_, ...), custom_call_target="tpu_custom_call", output_to_operand_aliasing={{}: (0, {})} | custom-call | flops 1073741824 | bytes 1048576 | tf_op jit(solution)/shard_map/grad_out/pallas_call | solution.py:384
  134.5 8.9 %collective-permute-done.30.refs_2_ = bf16[64,2048]{1,0:T(8,128)(2,1)S(1)} collective-permute-done((bf16[64,2048]{1,0:T(8,128)(2,1)S(1)}, bf16[64,2048]{1,0:T(8,128)(2,1)S(1)}, u32[]{:S(2)}, u32[]{:S(2)}) %collective-permute-start.30) | collective-permute-done | bytes 262176 | tf_op jit(solution)/shard_map/ppermute | solution.py:281
  143.5 1.5 %last.1 = (bf16[128,1024]{1,0:T(8,128)(2,1)}, bf16[128,1024]{1,0:T(8,128)(2,1)}) custom-call(s32[128,2]{1,0:T(8,128)S(1)} %get-tuple-element.44.slot_ref, bf16[128,1024]{1,0:T(8,128)(2,1)S(1)} %copy-done, f32[1,1024]{1,0:T(1,128)S(1)} %bitcast.9, f32[128,2]{1,0:T(8,128)S(1)} %get-tuple-element.45.gate_ref, bf16[128,1024]{1,0:T(8,128)(2,1)S(1)} %copy-done.1, ...), custom_call_target="tpu_custom_call" | custom-call | tf_op jit(solution)/shard_map/last/pallas_call | solution.py:405
  (84 shorter events, 1.6 us)
Async XLA Ops:
  2.6 2.1 %collective-permute-start = (bf16[128,2048]{1,0:T(8,128)(2,1)S(1)}, bf16[128,2048]{1,0:T(8,128)(2,1)S(1)}, u32[]{:S(2)}, u32[]{:S(2)}) collective-permute-start(bf16[128,2048]{1,0:T(8,128)(2,1)S(1)} %get-tuple-element.47), channel_id=1, source_target_pairs={{0,1},{1,0},{2,3},{3,2},{4,5},{5,4},{6,7},{7,6},{8,9},{9,8},{10,11... | collective-permute-start | bytes 1572872 | tf_op jit(solution)/shard_map/ppermute | solution.py:281
  3.1 33.2 %copy-start.4 = (bf16[1,1024,1024]{2,1,0:T(8,128)(2,1)S(1)}, bf16[1,1024,1024]{2,1,0:T(8,128)(2,1)}, u32[]{:S(2)}) copy-start(bf16[1,1024,1024]{2,1,0:T(8,128)(2,1)} %param.12) | copy-start | bytes 6291460
  3.2 33.1 %copy-start.3 = (bf16[1,1024,1024]{2,1,0:T(8,128)(2,1)S(1)}, bf16[1,1024,1024]{2,1,0:T(8,128)(2,1)}, u32[]{:S(2)}) copy-start(bf16[1,1024,1024]{2,1,0:T(8,128)(2,1)} %param.11) | copy-start | bytes 6291460
  4.7 9.5 %collective-permute-start.2 = (bf16[64,2048]{1,0:T(8,128)(2,1)S(1)}, bf16[64,2048]{1,0:T(8,128)(2,1)S(1)}, u32[]{:S(2)}, u32[]{:S(2)}) collective-permute-start(bf16[64,2048]{1,0:T(8,128)(2,1)S(1)} %pad_maximum_fusion.refs_0_), channel_id=1, source_target_pairs={{0,16},{8,24},{16,0},{24,8},{1,17},{9,25},{17,1},{25,9},{2,18},{10... | collective-permute-start | bytes 786440 | tf_op jit(solution)/shard_map/ppermute | solution.py:281
  7.7 8.4 %collective-permute-start.1 = (bf16[64,2048]{1,0:T(8,128)(2,1)S(1)}, bf16[64,2048]{1,0:T(8,128)(2,1)S(1)}, u32[]{:S(2)}, u32[]{:S(2)}) collective-permute-start(bf16[64,2048]{1,0:T(8,128)(2,1)S(1)} %pad_maximum_fusion.refs_0_), channel_id=1, source_target_pairs={{0,8},{8,0},{16,24},{24,16},{1,9},{9,1},{17,25},{25,17},{2,10},{10... | collective-permute-start | bytes 786440 | tf_op jit(solution)/shard_map/ppermute | solution.py:281
  9.2 12.6 %collective-permute-start.10 = (bf16[64,2048]{1,0:T(8,128)(2,1)S(1)}, bf16[64,2048]{1,0:T(8,128)(2,1)S(1)}, u32[]{:S(2)}, u32[]{:S(2)}) collective-permute-start(bf16[64,2048]{1,0:T(8,128)(2,1)S(1)} %pad_maximum_fusion.1), channel_id=1, source_target_pairs={{0,2},{1,3},{2,0},{3,1},{4,6},{5,7},{6,4},{7,5},{8,10},{9,11},{10,... | collective-permute-start | bytes 786440 | tf_op jit(solution)/shard_map/ppermute | solution.py:281
  10.9 21.4 %collective-permute-start.20 = (bf16[64,2048]{1,0:T(8,128)(2,1)S(1)}, bf16[64,2048]{1,0:T(8,128)(2,1)S(1)}, u32[]{:S(2)}, u32[]{:S(2)}) collective-permute-start(bf16[64,2048]{1,0:T(8,128)(2,1)S(1)} %pad_maximum_fusion.2), channel_id=1, source_target_pairs={{0,4},{1,5},{2,6},{3,7},{4,0},{5,1},{6,2},{7,3},{8,12},{9,13},{10,... | collective-permute-start | bytes 786440 | tf_op jit(solution)/shard_map/ppermute | solution.py:281
  13.5 19.2 %collective-permute-start.31 = (bf16[64,2048]{1,0:T(8,128)(2,1)S(1)}, bf16[64,2048]{1,0:T(8,128)(2,1)S(1)}, u32[]{:S(2)}, u32[]{:S(2)}) collective-permute-start(bf16[64,2048]{1,0:T(8,128)(2,1)S(1)} %pad_maximum_fusion.3), channel_id=1, source_target_pairs={{0,6},{1,7},{2,4},{3,5},{4,2},{5,3},{6,0},{7,1},{8,14},{9,15},{10,... | collective-permute-start | bytes 786440 | tf_op jit(solution)/shard_map/ppermute | solution.py:281
  14.3 19.0 %collective-permute-start.3 = (bf16[32,2048]{1,0:T(8,128)(2,1)S(1)}, bf16[32,2048]{1,0:T(8,128)(2,1)S(1)}, u32[]{:S(2)}, u32[]{:S(2)}) collective-permute-start(bf16[32,2048]{1,0:T(8,128)(2,1)S(1)} %slice.161), channel_id=1, source_target_pairs={{0,8},{8,0},{16,24},{24,16},{1,9},{9,1},{17,25},{25,17},{2,10},{10... | collective-permute-start | bytes 393224 | tf_op jit(solution)/shard_map/ppermute | solution.py:281
  16.1 18.7 %collective-permute-start.4 = (bf16[32,2048]{1,0:T(8,128)(2,1)S(1)}, bf16[32,2048]{1,0:T(8,128)(2,1)S(1)}, u32[]{:S(2)}, u32[]{:S(2)}) collective-permute-start(bf16[32,2048]{1,0:T(8,128)(2,1)S(1)} %slice.162), channel_id=1, source_target_pairs={{0,16},{8,24},{16,0},{24,8},{1,17},{9,25},{17,1},{25,9},{2,18},{10... | collective-permute-start | bytes 393224 | tf_op jit(solution)/shard_map/ppermute | solution.py:281
  21.7 17.2 %collective-permute-start.12 = (bf16[64,2048]{1,0:T(8,128)(2,1)S(1)}, bf16[64,2048]{1,0:T(8,128)(2,1)S(1)}, u32[]{:S(2)}, u32[]{:S(2)}) collective-permute-start(bf16[64,2048]{1,0:T(8,128)(2,1)S(1)} %collective-permute-done.10.refs_0_), channel_id=1, source_target_pairs={{0,16},{8,24},{16,0},{24,8},{1,17},{9,25},{17,1},{25,9},{2,18},{10... | collective-permute-start | bytes 786440 | tf_op jit(solution)/shard_map/ppermute | solution.py:281
  32.2 8.8 %collective-permute-start.11 = (bf16[64,2048]{1,0:T(8,128)(2,1)S(1)}, bf16[64,2048]{1,0:T(8,128)(2,1)S(1)}, u32[]{:S(2)}, u32[]{:S(2)}) collective-permute-start(bf16[64,2048]{1,0:T(8,128)(2,1)S(1)} %collective-permute-done.10.refs_0_), channel_id=1, source_target_pairs={{0,8},{8,0},{16,24},{24,16},{1,9},{9,1},{17,25},{25,17},{2,10},{10... | collective-permute-start | bytes 786440 | tf_op jit(solution)/shard_map/ppermute | solution.py:281
  32.8 8.3 %collective-permute-start.22 = (bf16[64,2048]{1,0:T(8,128)(2,1)S(1)}, bf16[64,2048]{1,0:T(8,128)(2,1)S(1)}, u32[]{:S(2)}, u32[]{:S(2)}) collective-permute-start(bf16[64,2048]{1,0:T(8,128)(2,1)S(1)} %collective-permute-done.20.refs_0_), channel_id=1, source_target_pairs={{0,16},{8,24},{16,0},{24,8},{1,17},{9,25},{17,1},{25,9},{2,18},{10... | collective-permute-start | bytes 786440 | tf_op jit(solution)/shard_map/ppermute | solution.py:281
  33.3 13.4 %collective-permute-start.21 = (bf16[64,2048]{1,0:T(8,128)(2,1)S(1)}, bf16[64,2048]{1,0:T(8,128)(2,1)S(1)}, u32[]{:S(2)}, u32[]{:S(2)}) collective-permute-start(bf16[64,2048]{1,0:T(8,128)(2,1)S(1)} %collective-permute-done.20.refs_0_), channel_id=1, source_target_pairs={{0,8},{8,0},{16,24},{24,16},{1,9},{9,1},{17,25},{25,17},{2,10},{10... | collective-permute-start | bytes 786440 | tf_op jit(solution)/shard_map/ppermute | solution.py:281
  34.8 11.9 %collective-permute-start.33 = (bf16[64,2048]{1,0:T(8,128)(2,1)S(1)}, bf16[64,2048]{1,0:T(8,128)(2,1)S(1)}, u32[]{:S(2)}, u32[]{:S(2)}) collective-permute-start(bf16[64,2048]{1,0:T(8,128)(2,1)S(1)} %collective-permute-done.31.refs_0_), channel_id=1, source_target_pairs={{0,16},{8,24},{16,0},{24,8},{1,17},{9,25},{17,1},{25,9},{2,18},{10... | collective-permute-start | bytes 786440 | tf_op jit(solution)/shard_map/ppermute | solution.py:281
  39.0 13.3 %collective-permute-start.32 = (bf16[64,2048]{1,0:T(8,128)(2,1)S(1)}, bf16[64,2048]{1,0:T(8,128)(2,1)S(1)}, u32[]{:S(2)}, u32[]{:S(2)}) collective-permute-start(bf16[64,2048]{1,0:T(8,128)(2,1)S(1)} %collective-permute-done.31.refs_0_), channel_id=1, source_target_pairs={{0,8},{8,0},{16,24},{24,16},{1,9},{9,1},{17,25},{25,17},{2,10},{10... | collective-permute-start | bytes 786440 | tf_op jit(solution)/shard_map/ppermute | solution.py:281
  41.1 14.4 %collective-permute-start.6 = (bf16[64,2048]{1,0:T(8,128)(2,1)S(1)}, bf16[64,2048]{1,0:T(8,128)(2,1)S(1)}, u32[]{:S(2)}, u32[]{:S(2)}) collective-permute-start(bf16[64,2048]{1,0:T(8,128)(2,1)S(1)} %get-tuple-element.50), channel_id=1, source_target_pairs={{0,8},{8,0},{16,24},{24,16},{1,9},{9,1},{17,25},{25,17},{2,10},{10... | collective-permute-start | bytes 786440 | tf_op jit(solution)/shard_map/ppermute | solution.py:281
  41.1 40.1 %collective-permute-start.5 = (bf16[128,2048]{1,0:T(8,128)(2,1)S(1)}, bf16[128,2048]{1,0:T(8,128)(2,1)S(1)}, u32[]{:S(2)}, u32[]{:S(2)}) collective-permute-start(bf16[128,2048]{1,0:T(8,128)(2,1)S(1)} %get-tuple-element.49), channel_id=1, source_target_pairs={{0,1},{1,0},{2,3},{3,2},{4,5},{5,4},{6,7},{7,6},{8,9},{9,8},{10,11... | collective-permute-start | bytes 1572872 | tf_op jit(solution)/shard_map/ppermute | solution.py:281
  46.7 22.9 %collective-permute-start.13 = (bf16[32,2048]{1,0:T(8,128)(2,1)S(1)}, bf16[32,2048]{1,0:T(8,128)(2,1)S(1)}, u32[]{:S(2)}, u32[]{:S(2)}) collective-permute-start(bf16[32,2048]{1,0:T(8,128)(2,1)S(1)} %slice.171), channel_id=1, source_target_pairs={{0,8},{8,0},{16,24},{24,16},{1,9},{9,1},{17,25},{25,17},{2,10},{10... | collective-permute-start | bytes 393224 | tf_op jit(solution)/shard_map/ppermute | solution.py:281
  46.7 23.0 %collective-permute-start.14 = (bf16[32,2048]{1,0:T(8,128)(2,1)S(1)}, bf16[32,2048]{1,0:T(8,128)(2,1)S(1)}, u32[]{:S(2)}, u32[]{:S(2)}) collective-permute-start(bf16[32,2048]{1,0:T(8,128)(2,1)S(1)} %slice.172), channel_id=1, source_target_pairs={{0,16},{8,24},{16,0},{24,8},{1,17},{9,25},{17,1},{25,9},{2,18},{10... | collective-permute-start | bytes 393224 | tf_op jit(solution)/shard_map/ppermute | solution.py:281
  52.3 7.4 %collective-permute-start.23 = (bf16[32,2048]{1,0:T(8,128)(2,1)S(1)}, bf16[32,2048]{1,0:T(8,128)(2,1)S(1)}, u32[]{:S(2)}, u32[]{:S(2)}) collective-permute-start(bf16[32,2048]{1,0:T(8,128)(2,1)S(1)} %slice.178), channel_id=1, source_target_pairs={{0,8},{8,0},{16,24},{24,16},{1,9},{9,1},{17,25},{25,17},{2,10},{10... | collective-permute-start | bytes 393224 | tf_op jit(solution)/shard_map/ppermute | solution.py:281
  55.5 5.0 %collective-permute-start.24 = (bf16[32,2048]{1,0:T(8,128)(2,1)S(1)}, bf16[32,2048]{1,0:T(8,128)(2,1)S(1)}, u32[]{:S(2)}, u32[]{:S(2)}) collective-permute-start(bf16[32,2048]{1,0:T(8,128)(2,1)S(1)} %slice.179), channel_id=1, source_target_pairs={{0,16},{8,24},{16,0},{24,8},{1,17},{9,25},{17,1},{25,9},{2,18},{10... | collective-permute-start | bytes 393224 | tf_op jit(solution)/shard_map/ppermute | solution.py:281
  59.7 6.0 %collective-permute-start.34 = (bf16[32,2048]{1,0:T(8,128)(2,1)S(1)}, bf16[32,2048]{1,0:T(8,128)(2,1)S(1)}, u32[]{:S(2)}, u32[]{:S(2)}) collective-permute-start(bf16[32,2048]{1,0:T(8,128)(2,1)S(1)} %slice.188), channel_id=1, source_target_pairs={{0,8},{8,0},{16,24},{24,16},{1,9},{9,1},{17,25},{25,17},{2,10},{10... | collective-permute-start | bytes 393224 | tf_op jit(solution)/shard_map/ppermute | solution.py:281
  60.4 6.1 %collective-permute-start.35 = (bf16[32,2048]{1,0:T(8,128)(2,1)S(1)}, bf16[32,2048]{1,0:T(8,128)(2,1)S(1)}, u32[]{:S(2)}, u32[]{:S(2)}) collective-permute-start(bf16[32,2048]{1,0:T(8,128)(2,1)S(1)} %slice.189), channel_id=1, source_target_pairs={{0,16},{8,24},{16,0},{24,8},{1,17},{9,25},{17,1},{25,9},{2,18},{10... | collective-permute-start | bytes 393224 | tf_op jit(solution)/shard_map/ppermute | solution.py:281
  65.7 68.7 %collective-permute-start.8 = (bf16[32,2048]{1,0:T(8,128)(2,1)S(1)}, bf16[32,2048]{1,0:T(8,128)(2,1)S(1)}, u32[]{:S(2)}, u32[]{:S(2)}) collective-permute-start(bf16[32,2048]{1,0:T(8,128)(2,1)S(1)} %add_convert_fusion.11), channel_id=1, source_target_pairs={{0,16},{8,24},{16,0},{24,8},{1,17},{9,25},{17,1},{25,9},{2,18},{10... | collective-permute-start | bytes 393224 | tf_op jit(solution)/shard_map/ppermute | solution.py:281
  66.6 15.8 %collective-permute-start.26 = (bf16[64,2048]{1,0:T(8,128)(2,1)S(1)}, bf16[64,2048]{1,0:T(8,128)(2,1)S(1)}, u32[]{:S(2)}, u32[]{:S(2)}) collective-permute-start(bf16[64,2048]{1,0:T(8,128)(2,1)S(1)} %get-tuple-element.59), channel_id=1, source_target_pairs={{0,8},{8,0},{16,24},{24,16},{1,9},{9,1},{17,25},{25,17},{2,10},{10... | collective-permute-start | bytes 786440 | tf_op jit(solution)/shard_map/ppermute | solution.py:281
  69.6 41.3 %collective-permute-start.25 = (bf16[128,2048]{1,0:T(8,128)(2,1)S(1)}, bf16[128,2048]{1,0:T(8,128)(2,1)S(1)}, u32[]{:S(2)}, u32[]{:S(2)}) collective-permute-start(bf16[128,2048]{1,0:T(8,128)(2,1)S(1)} %get-tuple-element.58), channel_id=1, source_target_pairs={{0,1},{1,0},{2,3},{3,2},{4,5},{5,4},{6,7},{7,6},{8,9},{9,8},{10,11... | collective-permute-start | bytes 1572872 | tf_op jit(solution)/shard_map/ppermute | solution.py:281
  69.7 13.7 %collective-permute-start.36 = (bf16[64,2048]{1,0:T(8,128)(2,1)S(1)}, bf16[64,2048]{1,0:T(8,128)(2,1)S(1)}, u32[]{:S(2)}, u32[]{:S(2)}) collective-permute-start(bf16[64,2048]{1,0:T(8,128)(2,1)S(1)} %get-tuple-element.62), channel_id=1, source_target_pairs={{0,8},{8,0},{16,24},{24,16},{1,9},{9,1},{17,25},{25,17},{2,10},{10... | collective-permute-start | bytes 786440 | tf_op jit(solution)/shard_map/ppermute | solution.py:281
  81.2 9.2 %collective-permute-start.37 = (bf16[64,2048]{1,0:T(8,128)(2,1)S(1)}, bf16[64,2048]{1,0:T(8,128)(2,1)S(1)}, u32[]{:S(2)}, u32[]{:S(2)}) collective-permute-start(bf16[64,2048]{1,0:T(8,128)(2,1)S(1)} %get-tuple-element.63), channel_id=1, source_target_pairs={{0,16},{8,24},{16,0},{24,8},{1,17},{9,25},{17,1},{25,9},{2,18},{10... | collective-permute-start | bytes 786440 | tf_op jit(solution)/shard_map/ppermute | solution.py:281
  82.4 23.4 %copy-start.5 = (bf16[64,2048]{1,0:T(8,128)(2,1)}, bf16[64,2048]{1,0:T(8,128)(2,1)S(1)}, u32[]{:S(2)}) copy-start(bf16[64,2048]{1,0:T(8,128)(2,1)S(1)} %collective-permute-done.26) | copy-start | bytes 786436
  82.4 9.2 %collective-permute-start.15 = (bf16[64,2048]{1,0:T(8,128)(2,1)S(1)}, bf16[64,2048]{1,0:T(8,128)(2,1)S(1)}, u32[]{:S(2)}, u32[]{:S(2)}) collective-permute-start(bf16[64,2048]{1,0:T(8,128)(2,1)S(1)} %get-tuple-element.53), channel_id=1, source_target_pairs={{0,8},{8,0},{16,24},{24,16},{1,9},{9,1},{17,25},{25,17},{2,10},{10... | collective-permute-start | bytes 786440 | tf_op jit(solution)/shard_map/ppermute | solution.py:281
  83.4 12.6 %collective-permute-start.16 = (bf16[64,2048]{1,0:T(8,128)(2,1)S(1)}, bf16[64,2048]{1,0:T(8,128)(2,1)S(1)}, u32[]{:S(2)}, u32[]{:S(2)}) collective-permute-start(bf16[64,2048]{1,0:T(8,128)(2,1)S(1)} %get-tuple-element.54), channel_id=1, source_target_pairs={{0,16},{8,24},{16,0},{24,8},{1,17},{9,25},{17,1},{25,9},{2,18},{10... | collective-permute-start | bytes 786440 | tf_op jit(solution)/shard_map/ppermute | solution.py:281
  90.4 22.9 %collective-permute-start.7 = (bf16[64,2048]{1,0:T(8,128)(2,1)S(1)}, bf16[64,2048]{1,0:T(8,128)(2,1)S(1)}, u32[]{:S(2)}, u32[]{:S(2)}) collective-permute-start(bf16[64,2048]{1,0:T(8,128)(2,1)S(1)} %slice.165), channel_id=1, source_target_pairs={{0,16},{8,24},{16,0},{24,8},{1,17},{9,25},{17,1},{25,9},{2,18},{10... | collective-permute-start | bytes 786440 | tf_op jit(solution)/shard_map/ppermute | solution.py:281
  91.6 12.0 %collective-permute-start.38 = (bf16[32,2048]{1,0:T(8,128)(2,1)S(1)}, bf16[32,2048]{1,0:T(8,128)(2,1)S(1)}, u32[]{:S(2)}, u32[]{:S(2)}) collective-permute-start(bf16[32,2048]{1,0:T(8,128)(2,1)S(1)} %add_convert_fusion.5), channel_id=1, source_target_pairs={{0,16},{8,24},{16,0},{24,8},{1,17},{9,25},{17,1},{25,9},{2,18},{10... | collective-permute-start | bytes 393224 | tf_op jit(solution)/shard_map/ppermute | solution.py:281
  96.0 8.7 %collective-permute-start.39 = (bf16[32,2048]{1,0:T(8,128)(2,1)S(1)}, bf16[32,2048]{1,0:T(8,128)(2,1)S(1)}, u32[]{:S(2)}, u32[]{:S(2)}) collective-permute-start(bf16[32,2048]{1,0:T(8,128)(2,1)S(1)} %add_convert_fusion.4), channel_id=1, source_target_pairs={{0,8},{8,0},{16,24},{24,16},{1,9},{9,1},{17,25},{25,17},{2,10},{10... | collective-permute-start | bytes 393224 | tf_op jit(solution)/shard_map/ppermute | solution.py:281
  103.6 5.0 %collective-permute-start.17 = (bf16[32,2048]{1,0:T(8,128)(2,1)S(1)}, bf16[32,2048]{1,0:T(8,128)(2,1)S(1)}, u32[]{:S(2)}, u32[]{:S(2)}) collective-permute-start(bf16[32,2048]{1,0:T(8,128)(2,1)S(1)} %add_convert_fusion.9), channel_id=1, source_target_pairs={{0,16},{8,24},{16,0},{24,8},{1,17},{9,25},{17,1},{25,9},{2,18},{10... | collective-permute-start | bytes 393224 | tf_op jit(solution)/shard_map/ppermute | solution.py:281
  104.7 5.0 %collective-permute-start.18 = (bf16[32,2048]{1,0:T(8,128)(2,1)S(1)}, bf16[32,2048]{1,0:T(8,128)(2,1)S(1)}, u32[]{:S(2)}, u32[]{:S(2)}) collective-permute-start(bf16[32,2048]{1,0:T(8,128)(2,1)S(1)} %add_convert_fusion.8), channel_id=1, source_target_pairs={{0,8},{8,0},{16,24},{24,16},{1,9},{9,1},{17,25},{25,17},{2,10},{10... | collective-permute-start | bytes 393224 | tf_op jit(solution)/shard_map/ppermute | solution.py:281
  108.6 19.9 %slice-start = ((bf16[64,2048]{1,0:T(8,128)(2,1)}), bf16[32,2048]{1,0:T(8,128)(2,1)S(1)}, s32[]{:S(2)}) async-start(bf16[64,2048]{1,0:T(8,128)(2,1)} %copy-done.5), calls=%async_computation | async-start | bytes 262144 | tf_op jit(solution)/shard_map/slice | solution.py:367
  108.6 16.1 %collective-permute-start.28 = (bf16[32,2048]{1,0:T(8,128)(2,1)S(1)}, bf16[32,2048]{1,0:T(8,128)(2,1)S(1)}, u32[]{:S(2)}, u32[]{:S(2)}) collective-permute-start(bf16[32,2048]{1,0:T(8,128)(2,1)S(1)} %add_convert_fusion.7), channel_id=1, source_target_pairs={{0,16},{8,24},{16,0},{24,8},{1,17},{9,25},{17,1},{25,9},{2,18},{10... | collective-permute-start | bytes 393224 | tf_op jit(solution)/shard_map/ppermute | solution.py:281
  109.7 11.0 %collective-permute-start.40 = (bf16[64,2048]{1,0:T(8,128)(2,1)S(1)}, bf16[64,2048]{1,0:T(8,128)(2,1)S(1)}, u32[]{:S(2)}, u32[]{:S(2)}) collective-permute-start(bf16[64,2048]{1,0:T(8,128)(2,1)S(1)} %add_convert_fusion), channel_id=1, source_target_pairs={{0,6},{1,7},{2,4},{3,5},{4,2},{5,3},{6,0},{7,1},{8,14},{9,15},{10,... | collective-permute-start | bytes 786440 | tf_op jit(solution)/shard_map/ppermute | solution.py:281
  110.9 12.3 %collective-permute-start.19 = (bf16[64,2048]{1,0:T(8,128)(2,1)S(1)}, bf16[64,2048]{1,0:T(8,128)(2,1)S(1)}, u32[]{:S(2)}, u32[]{:S(2)}) collective-permute-start(bf16[64,2048]{1,0:T(8,128)(2,1)S(1)} %add_convert_fusion.2), channel_id=1, source_target_pairs={{0,2},{1,3},{2,0},{3,1},{4,6},{5,7},{6,4},{7,5},{8,10},{9,11},{10,... | collective-permute-start | bytes 786440 | tf_op jit(solution)/shard_map/ppermute | solution.py:281
  113.3 9.9 %collective-permute-start.27 = (bf16[64,2048]{1,0:T(8,128)(2,1)S(1)}, bf16[64,2048]{1,0:T(8,128)(2,1)S(1)}, u32[]{:S(2)}, u32[]{:S(2)}) collective-permute-start(bf16[64,2048]{1,0:T(8,128)(2,1)S(1)} %slice.182), channel_id=1, source_target_pairs={{0,16},{8,24},{16,0},{24,8},{1,17},{9,25},{17,1},{25,9},{2,18},{10... | collective-permute-start | bytes 786440 | tf_op jit(solution)/shard_map/ppermute | solution.py:281
  120.7 13.7 %collective-permute-start.9 = (bf16[32,2048]{1,0:T(8,128)(2,1)S(1)}, bf16[32,2048]{1,0:T(8,128)(2,1)S(1)}, u32[]{:S(2)}, u32[]{:S(2)}) collective-permute-start(bf16[32,2048]{1,0:T(8,128)(2,1)S(1)} %add_convert_fusion.10), channel_id=1, source_target_pairs={{0,8},{8,0},{16,24},{24,16},{1,9},{9,1},{17,25},{25,17},{2,10},{10... | collective-permute-start | bytes 393224 | tf_op jit(solution)/shard_map/ppermute | solution.py:281
  123.3 5.2 %collective-permute-start.29 = (bf16[32,2048]{1,0:T(8,128)(2,1)S(1)}, bf16[32,2048]{1,0:T(8,128)(2,1)S(1)}, u32[]{:S(2)}, u32[]{:S(2)}) collective-permute-start(bf16[32,2048]{1,0:T(8,128)(2,1)S(1)} %add_convert_fusion.6), channel_id=1, source_target_pairs={{0,8},{8,0},{16,24},{24,16},{1,9},{9,1},{17,25},{25,17},{2,10},{10... | collective-permute-start | bytes 393224 | tf_op jit(solution)/shard_map/ppermute | solution.py:281
  124.6 9.9 %collective-permute-start.41 = (bf16[64,2048]{1,0:T(8,128)(2,1)S(1)}, bf16[64,2048]{1,0:T(8,128)(2,1)S(1)}, u32[]{:S(2)}, u32[]{:S(2)}) collective-permute-start(bf16[64,2048]{1,0:T(8,128)(2,1)S(1)} %pad_maximum_fusion.4), channel_id=1, source_target_pairs={{0,1},{1,0},{2,3},{3,2},{4,5},{5,4},{6,7},{7,6},{8,9},{9,8},{10,11... | collective-permute-start | bytes 786440 | tf_op jit(solution)/shard_map/ppermute | solution.py:281
  128.6 14.9 %copy-start = (bf16[128,1024]{1,0:T(8,128)(2,1)S(1)}, bf16[128,1024]{1,0:T(8,128)(2,1)}, u32[]{:S(2)}) copy-start(bf16[128,1024]{1,0:T(8,128)(2,1)} %tok_ref.1) | copy-start | bytes 786436
  128.6 14.9 %copy-start.1 = (bf16[128,1024]{1,0:T(8,128)(2,1)S(1)}, bf16[128,1024]{1,0:T(8,128)(2,1)}, u32[]{:S(2)}) copy-start(bf16[128,1024]{1,0:T(8,128)(2,1)} %cot_ref.1) | copy-start | bytes 786436
  128.6 14.8 %copy-start.2 = (f32[1024]{0:T(1024)S(1)}, f32[1024]{0:T(1024)}, u32[]{:S(2)}) copy-start(f32[1024]{0:T(1024)} %param.8) | copy-start | bytes 12292
  128.6 14.8 %collective-permute-start.30 = (bf16[64,2048]{1,0:T(8,128)(2,1)S(1)}, bf16[64,2048]{1,0:T(8,128)(2,1)S(1)}, u32[]{:S(2)}, u32[]{:S(2)}) collective-permute-start(bf16[64,2048]{1,0:T(8,128)(2,1)S(1)} %add_convert_fusion.1), channel_id=1, source_target_pairs={{0,4},{1,5},{2,6},{3,7},{4,0},{5,1},{6,2},{7,3},{8,12},{9,13},{10,... | collective-permute-start | bytes 786440 | tf_op jit(solution)/shard_map/ppermute | solution.py:281
